TPU v7x, 256 devices: a whole 4x4x8 slice. The times are simulated.
256 devices in a mesh: grp: 2 (over core), seq: 32 (over z, x), head: 4 (over y).
Axes of the slice: x: 4, y: 4, z: 8, core: 2. Of those that a mesh axis runs over, the one named last changes fastest.
Arguments:
- queries: bfloat16 [6144, 64, 128], P('seq', ('grp', 'head')), may hold values from -6 to 6
- keys: bfloat16 [6144, 64, 128], P('seq', ('grp', 'head')), may hold values from -6 to 6
- values: bfloat16 [6144, 64, 128], P('seq', ('grp', 'head')), may hold values from -6 to 6
- documents: int32 [6144], P('seq'), may hold values from 0 to 3, never falling along the last dimension, each value on 1 to 4608 neighbouring positions
- feature_map: float32 [64, 128, 128], P(('grp', 'head')), may hold values from -8 to 8
Outputs:
- teacher_out: bfloat16 [6144, 64, 128], P('seq', ('grp', 'head'))
- student_out: bfloat16 [6144, 64, 128], P('seq', ('grp', 'head'))
- loss: float32 [], replicated
- feature_grad: float32 [64, 128, 128], P(('grp', 'head'))
All inputs are finite; a program needn't handle non-finite values.
Results may differ from a plain program's by a relative error of at most 0.006.
Values may be sent and summed in bfloat16 or wider, within the bound.
A program may use at most 192 MiB of HBM per device.

v0:
```python
import functools

import jax
import jax.numpy as jnp
from jax import lax
from jax.sharding import Mesh
from jax.sharding import PartitionSpec as P

WINDOW = 64
SEQ = ("seq_0", "seq_1")
GRP_SEQ_HEAD = ("grp", "seq_0", "seq_1", "head")


exact_mode = lax.Precision.HIGHEST
masked_value = -1e30


def passed_along(block, axis, distance):
    devices = range(lax.axis_size(axis))
    route = [(i - distance, i) for i in devices if i - distance in devices]
    return lax.ppermute(block, axis, route)


def filled_with(array, identity):
    return jax.tree.map(
        lambda part, zero: jnp.zeros_like(part) + jnp.asarray(zero, part.dtype), array, identity
    )


def carried_in(array, axes, combine, identity, reverse):
    before = start = filled_with(array, identity)
    subtotal = array
    for axis in reversed(axes):
        peers, mine = (lax.axis_size(axis), lax.axis_index(axis))
        pieces = jax.tree.map(lambda part: lax.all_gather(part, axis), subtotal)
        inside, subtotal = (start, start)
        for k in reversed(range(peers)) if reverse else range(peers):
            passed = k > mine if reverse else k < mine
            subtotal = combine(subtotal, jax.tree.map(lambda part: part[k], pieces))
            inside = jax.tree.map(lambda new, old: jnp.where(passed, new, old), subtotal, inside)
        before = combine(inside, before)
    return before


def over_axes(array, axes):
    return functools.reduce(lax.psum, axes, array)


def features(inputs, weights):
    logits = jnp.einsum("rhd,hdf->rhf", inputs, weights, precision=exact_mode)
    return jnp.concatenate(
        [jax.nn.softmax(logits, axis=-1), jax.nn.softmax(-logits, axis=-1)], axis=-1
    )


def join_up(earlier, later):
    merged_tag = jnp.maximum(earlier[0], later[0])
    early_keep = (earlier[0] == merged_tag).astype(earlier[1].dtype)
    late_keep = (later[0] == merged_tag).astype(later[1].dtype)
    return (
        merged_tag,
        early_keep * earlier[1] + late_keep * later[1],
        early_keep * earlier[2] + late_keep * later[2],
    )


def join_down(earlier, later):
    merged_tag = jnp.minimum(earlier[0], later[0])
    early_keep = (earlier[0] == merged_tag).astype(earlier[1].dtype)
    late_keep = (later[0] == merged_tag).astype(later[1].dtype)
    return (
        merged_tag,
        early_keep * earlier[1] + late_keep * later[1],
        early_keep * earlier[2] + late_keep * later[2],
    )


def body(queries, keys, values, documents, feature_map):
    tok_rows, head_count, head_width = queries.shape
    half_feat = feature_map.shape[2] // 2
    score_scale = head_width ** (-0.5)
    seq_place = lax.axis_index(SEQ)
    seq_count = lax.axis_size(SEQ)
    first_row = seq_place * tok_rows
    doc_float = documents.astype(jnp.float32)
    doc_marks = (documents + 1).astype(jnp.bfloat16)
    query_pos = first_row + jnp.arange(tok_rows)
    key_piece = lax.all_gather(keys, SEQ, axis=0, tiled=True)
    value_piece = lax.all_gather(values, SEQ, axis=0, tiled=True)
    mark_piece = lax.all_gather(doc_marks, SEQ, axis=0, tiled=True)
    key_pos = jnp.arange(key_piece.shape[0])
    same_doc = mark_piece.astype(jnp.float32)[None, :] - 1.0 == doc_float[:, None]
    allowed = (same_doc & (key_pos[None, :] <= query_pos[:, None]))[:, None, :]
    scores = (
        jnp.einsum("ihd,jhd->ihj", queries, key_piece, preferred_element_type=jnp.float32)
        * score_scale
    )
    scores = jnp.where(allowed, scores, masked_value)
    row_max = jnp.full((tok_rows, head_count), masked_value, jnp.float32)
    new_max = jnp.maximum(row_max, jnp.max(scores, axis=-1))
    probabilities = jnp.where(allowed, jnp.exp(scores - new_max[:, :, None]), 0.0)
    totals = jnp.sum(probabilities, axis=-1)
    numerator = jnp.einsum(
        "ihj,jhd->ihd",
        probabilities.astype(jnp.bfloat16),
        value_piece,
        preferred_element_type=jnp.float32,
    )
    row_max, totals, numerator = (new_max, totals, numerator)
    teacher_out = (numerator / totals[:, :, None]).astype(jnp.bfloat16)
    target = teacher_out.astype(jnp.float32)
    halo_keys, halo_values, halo_marks = passed_along(
        (keys[tok_rows - WINDOW :], values[tok_rows - WINDOW :], doc_marks[tok_rows - WINDOW :]),
        SEQ,
        1,
    )
    key_joined = jnp.concatenate([halo_keys, keys], axis=0)
    key_float = key_joined.astype(jnp.float32)
    value_float = jnp.concatenate([halo_values, values], axis=0).astype(jnp.float32)
    doc_all = jnp.concatenate([halo_marks.astype(jnp.float32) - 1.0, doc_float], axis=0)
    query_float = queries.astype(jnp.float32)
    distance = jnp.arange(tok_rows)[:, None] + WINDOW - jnp.arange(tok_rows + WINDOW)[None, :]
    same_doc = doc_float[:, None] == doc_all[None, :]
    in_window = same_doc & (distance >= 0) & (distance < WINDOW)
    beyond = same_doc & (distance >= WINDOW)
    scores = (
        jnp.einsum("ihd,jhd->hij", queries, key_joined, preferred_element_type=jnp.float32)
        * score_scale
    )
    window_row = jnp.max(jnp.where(in_window[None], scores, masked_value), axis=-1, keepdims=True)
    window_weight = jnp.where(in_window[None], jnp.exp(scores - window_row), 0.0)
    elem_keys = key_float[:tok_rows]
    elem_values = value_float[:tok_rows]
    elem_docs = doc_all[:tok_rows]
    elem_tag = elem_docs[tok_rows - 1]
    in_tail = (elem_docs == elem_tag).astype(jnp.float32)

    def element(weights):
        masked_feat = features(elem_keys, weights[:, :, half_feat:]) * in_tail[:, None, None]
        return (
            jnp.einsum("jhf,jhd->hfd", masked_feat, elem_values, precision=exact_mode),
            jnp.sum(masked_feat, axis=0),
        )

    (elem_state, elem_norm), element_pullback = jax.vjp(element, feature_map)
    blank_state = jnp.zeros_like(elem_state)
    blank_norm = jnp.zeros_like(elem_norm)
    tag_in, state_in, norm_in = carried_in(
        (elem_tag, elem_state, elem_norm),
        SEQ,
        join_up,
        (jnp.float32(-2.0), blank_state, blank_norm),
        False,
    )
    uses_state = (doc_float == tag_in).astype(jnp.float32)[:, None]
    normaliser = 1.0 / (tok_rows * seq_count * head_count * lax.axis_size(("grp", "head")))

    def local_loss(weights, state, norm):
        query_feat = features(query_float, weights[:, :, :half_feat])
        key_feat = features(key_float, weights[:, :, half_feat:])
        linear = jnp.where(
            beyond[None],
            jnp.einsum("ihf,jhf->hij", query_feat, key_feat, precision=exact_mode),
            0.0,
        )
        weight = window_weight + linear
        numer_sum = jnp.einsum("hij,jhd->ihd", weight, value_float, precision=exact_mode)
        numer_sum = numer_sum + uses_state[:, :, None] * jnp.einsum(
            "ihf,hfd->ihd", query_feat, state, precision=exact_mode
        )
        denominator = jnp.sum(weight, axis=-1).T + uses_state * jnp.einsum(
            "ihf,hf->ih", query_feat, norm, precision=exact_mode
        )
        output = numer_sum / denominator[:, :, None]
        return (jnp.sum(jnp.square(output - target)) * normaliser, output)

    local_part, local_pullback, output = jax.vjp(
        local_loss, feature_map, state_in, norm_in, has_aux=True
    )
    grad_direct, grad_state, grad_norm = local_pullback(jnp.ones_like(local_part))
    back_tag, carried_state, carried_norm = carried_in(
        (tag_in, grad_state, grad_norm),
        SEQ,
        join_down,
        (jnp.float32(1000000000.0), blank_state, blank_norm),
        True,
    )
    total_grad = grad_direct + element_pullback((carried_state, carried_norm))[0]
    feature_grad = over_axes(total_grad, SEQ)
    loss_total = jax.tree.map(lambda part: over_axes(part, GRP_SEQ_HEAD), local_part)
    return (teacher_out, output.astype(jnp.bfloat16), loss_total, feature_grad)


def solution(mesh):
    split = Mesh(
        mesh.devices.reshape(mesh.shape["grp"], 8, 4, mesh.shape["head"]),
        ("grp", "seq_0", "seq_1", "head"),
    )
    return jax.shard_map(
        body,
        mesh=split,
        in_specs=(
            P(SEQ, ("grp", "head"), None),
            P(SEQ, ("grp", "head"), None),
            P(SEQ, ("grp", "head"), None),
            P(SEQ),
            P(("grp", "head"), None, None),
        ),
        out_specs=(
            P(SEQ, ("grp", "head"), None),
            P(SEQ, ("grp", "head"), None),
            P(),
            P(("grp", "head"), None, None),
        ),
        check_vma=False,
    )
```

profile of v0, /device:TPU:32, one launch (start us, length us, event | category | flops | bytes accessed | tf_op | source)
XLA Modules:
  0.0 641.0 jit_solution(11608733308166562102)
XLA Ops:
  7.3 1.1 copy.34
  8.4 3.4 collective-permute-start.2
  12.6 3.4 collective-permute-start.1
  16.0 1.1 copy.36
  17.1 3.1 collective-permute-start
  20.8 1.2 slice_dynamic-update-slice_fusion
  23.0 1.0 convolution_bitcast_fusion.1
  27.3 1.5 fusion.37
  28.9 11.0 %all-reduce.4 = f32[4]{0:T(128)S(1)} all-reduce(f32[4]{0:T(128)S(1)} %get-tuple-element.28), channel_id=1, replica_groups=mesh['grp'=2,'seq_0'=8,'seq_1'=4,'head'=4] {'seq_1'}, use_global_device_ids=true, to_apply=%add.4 | all-reduce | flops 4 | bytes 32
  45.8 18.4 %all-gather.19.cloned.1.call-done = f32[32,128,128]{2,1,0:T(8,128)} async-done(((f32[8,128,128]{2,1,0:T(8,128)}), f32[32,128,128]{2,1,0:T(8,128)}) %all-gather.19.cloned.1.call-update) | async-done | bytes 2097168 | tf_op jit(solution)/shard_map/all_gather | solution.py:35
  64.2 2.5 fusion.75
  69.5 16.2 %all-reduce.5 = f32[8]{0:T(128)S(1)} all-reduce(f32[8]{0:T(128)S(1)} %dynamic-update-slice.2), channel_id=1, replica_groups=mesh['grp'=2,'seq_0'=8,'seq_1'=4,'head'=4] {'seq_0'}, use_global_device_ids=true, to_apply=%add.5 | all-reduce | flops 8 | bytes 64
  98.3 137.4 %all-reduce.3 = bf16[6144]{0:T(1024)(128)(2,1)S(1)} all-reduce(bf16[6144]{0:T(1024)(128)(2,1)S(1)} %dynamic-update-slice), channel_id=1, replica_groups=mesh['grp'=2,'seq_0'=8,'seq_1'=4,'head'=4] {'seq_0','seq_1'}, use_global_device_ids=true, to_apply=%add.3 | all-reduce | flops 6144 | bytes 24576
  236.6 0.9 fusion.273
  239.4 1.0 fusion.13
  240.9 12.0 %all-gather.1 = f32[32,128]{1,0:T(8,128)S(1)} all-gather(f32[8,128]{1,0:T(8,128)S(1)} %fusion.36), channel_id=3, replica_groups=mesh['grp'=2,'seq_0'=8,'seq_1'=4,'head'=4] {'seq_1'}, dimensions={0}, use_global_device_ids=true | all-gather | bytes 20480 | tf_op jit(solution)/shard_map/all_gather | solution.py:35
  252.9 28.7 %all_gather.81 = f32[8,8,128]{2,1,0:T(8,128)S(1)} all-gather(f32[1,8,128]{2,1,0:T(8,128)S(1)} %fusion.245), channel_id=1, replica_groups=mesh['grp'=2,'seq_0'=8,'seq_1'=4,'head'=4] {'seq_0'}, dimensions={0}, use_global_device_ids=true | all-gather | bytes 36864 | tf_op jit(solution)/shard_map/all_gather | solution.py:35
  281.6 0.9 convolution_bitcast_fusion.2
  285.1 2.0 fusion.35
  288.3 2.0 fusion.277
  290.3 3.7 fusion.67
  294.7 2.7 convolution_multiply_fusion.1
  297.5 18.4 %fusion.7 = (f32[192,8]{0,1:T(8,128)S(1)}, f32[8,6144,192]{1,2,0:T(8,128)}) fusion(pred[192,6144]{1,0:T(8,128)(4,1)S(1)} %fusion.13, bf16[6144,8,128]{2,0,1:T(8,128)(2,1)} %all-gather.11.cloned.1.call-done, bf16[192,8,128]{2,1,0:T(8,128)(2,1)S(1)} %copy-done), kind=kOutput, calls=%fused_computation.9 | convolution fusion | flops 2444229120 | bytes 51910656 | tf_op jit(solution)/shard_map/ihd,jhd->ihj/dot_general | solution.py:95
  315.9 19.2 %fusion.8 = f32[192,8]{0,1:T(8,128)S(1)} fusion(f32[8,6144,192]{1,2,0:T(8,128)} %get-tuple-element.71, f32[192,8]{0,1:T(8,128)S(1)} %broadcast_maximum_fusion, pred[192,6144]{1,0:T(8,128)(4,1)S(1)} %fusion.13), kind=kLoop, calls=%fused_computation.10 | loop fusion | flops 47184384 | bytes 38940672 | tf_op jit(solution)/shard_map/reduce_sum | solution.py:102
  335.1 25.6 %all-gather.13.cloned.1.call-done = bf16[6144,8,128]{2,0,1:T(8,128)(2,1)} async-done(((bf16[192,8,128]{2,0,1:T(8,128)(2,1)}), bf16[6144,8,128]{2,0,1:T(8,128)(2,1)}) %all-gather.13.cloned.1.call-update) | async-done | bytes 12582928 | tf_op jit(solution)/shard_map/all_gather | solution.py:89
  360.8 21.6 %fusion.10 = f32[8,192,128]{2,1,0:T(8,128)} fusion(bf16[6144,8,128]{2,0,1:T(8,128)(2,1)} %all-gather.13.cloned.1.call-done, f32[8,6144,192]{1,2,0:T(8,128)} %get-tuple-element.71, f32[192,8]{0,1:T(8,128)S(1)} %broadcast_maximum_fusion, pred[192,6144]{1,0:T(8,128)(4,1)S(1)} %fusion.13), kind=kOutput, calls=%fused_computation.12 | convolution fusion | flops 2463105024 | bytes 52303872 | tf_op jit(solution)/shard_map/ihj,jhd->ihd/dot_general | solution.py:103
  382.4 3.7 fusion.40
  386.6 2.0 fusion.44
  389.4 8.5 %all-reduce.6 = f32[4]{0:T(128)S(1)} all-reduce(f32[4]{0:T(128)S(1)} %dynamic-update-slice.3), channel_id=1, replica_groups=mesh['grp'=2,'seq_0'=8,'seq_1'=4,'head'=4] {'seq_1'}, use_global_device_ids=true, to_apply=%add.6 | all-reduce | flops 4 | bytes 32
  403.5 17.4 %all-gather.21.cloned.1.call-done = f32[32,128,128]{2,1,0:T(8,128)} async-done(((f32[8,128,128]{2,1,0:T(8,128)}), f32[32,128,128]{2,1,0:T(8,128)}) %all-gather.21.cloned.1.call-update) | async-done | bytes 2097168 | tf_op jit(solution)/shard_map/all_gather | solution.py:35
  420.9 2.5 fusion.60
  425.6 3.0 psum.42
  428.5 17.5 %all-reduce.8 = (f32[]{:T(128)}, f32[8]{0:T(128)S(1)}) all-reduce(f32[]{:T(128)} %psum.42, f32[8]{0:T(128)S(1)} %dynamic-update-slice.4), channel_id=1, replica_groups=mesh['grp'=2,'seq_0'=8,'seq_1'=4,'head'=4] {'seq_0'}, use_global_device_ids=true, to_apply=%region_19.20 | all-reduce | flops 9 | bytes 72 | tf_op jit(solution)/shard_map/psum | solution.py:46
  456.6 2.0 add_select_fusion
  458.6 1.9 fusion.34
  460.6 1.8 fusion.21
  462.7 1.3 convolution_bitcast_fusion
  464.3 0.9 fusion.213
  465.2 12.0 %all-gather.2 = f32[32,128]{1,0:T(8,128)S(1)} all-gather(f32[8,128]{1,0:T(8,128)S(1)} %bitcast.225), channel_id=4, replica_groups=mesh['grp'=2,'seq_0'=8,'seq_1'=4,'head'=4] {'seq_1'}, dimensions={0}, use_global_device_ids=true | all-gather | bytes 20480 | tf_op jit(solution)/shard_map/all_gather | solution.py:35
  477.2 24.1 %all_gather.88 = f32[8,8,128]{2,1,0:T(8,128)S(1)} all-gather(f32[1,8,128]{2,1,0:T(8,128)S(1)} %fusion.230), channel_id=1, replica_groups=mesh['grp'=2,'seq_0'=8,'seq_1'=4,'head'=4] {'seq_0'}, dimensions={0}, use_global_device_ids=true | all-gather | bytes 36864 | tf_op jit(solution)/shard_map/all_gather | solution.py:35
  503.9 4.1 fusion.19
  509.9 72.6 %all-reduce.12.cloned.1.call-done = f32[8,128,128]{1,2,0:T(8,128)} async-done(((f32[8,128,128]{1,2,0:T(8,128)}), f32[8,128,128]{1,2,0:T(8,128)}) %all-reduce.12.cloned.1.call-update) | async-done | bytes 524304 | tf_op jit(solution)/shard_map/psum | solution.py:46
  582.5 11.1 %psum.44 = f32[]{:T(128)} all-reduce(f32[]{:T(128)} %get-tuple-element.20), channel_id=1, replica_groups=mesh['grp'=2,'seq_0'=8,'seq_1'=4,'head'=4] {'seq_1'}, use_global_device_ids=true, to_apply=%region_20.21 | all-reduce | flops 1 | bytes 8 | tf_op jit(solution)/shard_map/psum | solution.py:46
  593.6 11.1 %psum.45 = f32[]{:T(128)} all-reduce(f32[]{:T(128)} %psum.44), channel_id=1, replica_groups=mesh['grp'=2,'seq_0'=8,'seq_1'=4,'head'=4] {'head'}, use_global_device_ids=true, to_apply=%region_21.22 | all-reduce | flops 1 | bytes 8 | tf_op jit(solution)/shard_map/psum | solution.py:46
  604.6 1.0 copy.56
  605.6 1.0 copy.57
  606.6 25.0 %all-reduce.14.cloned.1.call-done = f32[8,128,128]{1,2,0:T(8,128)} async-done(((f32[8,128,128]{1,2,0:T(8,128)}), f32[8,128,128]{1,2,0:T(8,128)}) %all-reduce.14.cloned.1.call-update) | async-done | bytes 524304 | tf_op jit(solution)/shard_map/psum | solution.py:46
  631.6 2.0 copy.58
  (200 shorter events, 26.9 us)
Async XLA Ops:
  7.2 228.6 %copy-start = (bf16[192,8,128]{2,1,0:T(8,128)(2,1)S(1)}, bf16[192,8,128]{2,1,0:T(8,128)(2,1)}, u32[]{:S(2)}) copy-start(bf16[192,8,128]{2,1,0:T(8,128)(2,1)} %param.5) | copy-start | bytes 1179652
  7.2 13.0 %copy-start.53 = (u32[256]{0:T(256)S(1)}, u32[256]{0:T(256)}, u32[]{:S(2)}) copy-start(u32[256]{0:T(256)} %constant.93) | copy-start | bytes 3076
  7.2 15.7 %copy-start.31 = (bf16[192,8,128]{2,1,0:T(8,128)(2,1)S(1)}, bf16[192,8,128]{2,1,0:T(8,128)(2,1)}, u32[]{:S(2)}) copy-start(bf16[192,8,128]{2,1,0:T(8,128)(2,1)} %param.6) | copy-start | bytes 1179652
  7.2 15.8 %copy-start.11 = (f32[8,128,128]{2,1,0:T(8,128)S(1)}, f32[8,128,128]{2,1,0:T(8,128)}, u32[]{:S(2)}) copy-start(f32[8,128,128]{2,1,0:T(8,128)} %param.9) | copy-start | bytes 1572868
  7.2 57.0 %all-gather.19.cloned.1.call-start = ((), (), s32[]{:S(2)}) async-start(), calls=%async_computation.6 | async-start | bytes 2621440 | tf_op jit(solution)/shard_map/all_gather | solution.py:35
  8.4 16.6 %copy-start.25 = (bf16[192,8,128]{2,0,1:T(8,128)(2,1)}, bf16[192,8,128]{2,0,1:T(8,128)(2,1)S(1)}, u32[]{:S(2)}) copy-start(bf16[192,8,128]{2,0,1:T(8,128)(2,1)S(1)} %copy.34) | copy-start | bytes 1179652
  8.4 14.4 %collective-permute-start.2 = (bf16[64,8,128]{2,0,1:T(8,128)(2,1)S(1)}, bf16[64,8,128]{2,0,1:T(8,128)(2,1)S(1)}, u32[]{:S(2)}, u32[]{:S(2)}) collective-permute-start(bf16[64,8,128]{2,0,1:T(8,128)(2,1)S(1)} %slice.344), channel_id=1, source_target_pairs={{0,4},{4,8},{8,12},{12,16},{16,20},{20,24},{24,28},{28,32},{32,36}... | collective-permute-start | bytes 393224 | tf_op jit(solution)/shard_map/ppermute | solution.py:21
  12.6 10.2 %copy-start.44 = (f32[192]{0:T(256)}, f32[192]{0:T(256)S(1)}, u32[]{:S(2)}) copy-start(f32[192]{0:T(256)S(1)} %get-tuple-element.31) | copy-start | bytes 2308
  12.6 9.5 %collective-permute-start.1 = (bf16[64]{0:T(256)(128)(2,1)S(1)}, bf16[64]{0:T(256)(128)(2,1)S(1)}, u32[]{:S(2)}, u32[]{:S(2)}) collective-permute-start(bf16[64]{0:T(256)(128)(2,1)S(1)} %slice.247), channel_id=1, source_target_pairs={{0,4},{4,8},{8,12},{12,16},{16,20},{20,24},{24,28},{28,32},{32,36}... | collective-permute-start | bytes 392 | tf_op jit(solution)/shard_map/ppermute | solution.py:21
  17.1 8.8 %copy-start.26 = (bf16[192,8,128]{2,0,1:T(8,128)(2,1)}, bf16[192,8,128]{2,0,1:T(8,128)(2,1)S(1)}, u32[]{:S(2)}) copy-start(bf16[192,8,128]{2,0,1:T(8,128)(2,1)S(1)} %copy.36) | copy-start | bytes 1179652
  17.1 9.0 %collective-permute-start = (bf16[64,8,128]{2,0,1:T(8,128)(2,1)S(1)}, bf16[64,8,128]{2,0,1:T(8,128)(2,1)S(1)}, u32[]{:S(2)}, u32[]{:S(2)}) collective-permute-start(bf16[64,8,128]{2,0,1:T(8,128)(2,1)S(1)} %slice.343), channel_id=1, source_target_pairs={{0,4},{4,8},{8,12},{12,16},{16,20},{20,24},{24,28},{28,32},{32,36}... | collective-permute-start | bytes 393224 | tf_op jit(solution)/shard_map/ppermute | solution.py:21
  22.8 3.9 copy-start.46
  23.0 3.1 copy-start.32
  28.8 39.3 %copy-start.52 = (u32[256]{0:T(256)S(1)}, u32[256]{0:T(256)}, u32[]{:S(2)}) copy-start(u32[256]{0:T(256)} %constant.98) | copy-start | bytes 3076
  28.8 261.4 %all-gather.15.cloned.1.call-start = ((), (), s32[]{:S(2)}) async-start(), calls=%async_computation.2 | async-start | bytes 4718592 | tf_op jit(solution)/shard_map/all_gather | solution.py:35
  40.6 56.2 %copy-start.51 = (u32[256]{0:T(256)S(1)}, u32[256]{0:T(256)}, u32[]{:S(2)}) copy-start(u32[256]{0:T(256)} %constant.88) | copy-start | bytes 3076
  45.8 189.9 %copy-start.50 = (s32[192]{0:T(256)S(1)}, s32[192]{0:T(256)}, u32[]{:S(2)}) copy-start(s32[192]{0:T(256)} %param.8) | copy-start | bytes 2308
  66.7 230.7 %all-gather.11.cloned.1.call-start = ((), (), s32[]{:S(2)}) async-start(), calls=%async_computation | async-start | bytes 12976128 | tf_op jit(solution)/shard_map/all_gather | solution.py:88
  67.5 293.3 %all-gather.13.cloned.1.call-start = ((), (), s32[]{:S(2)}) async-start(), calls=%async_computation.1 | async-start | bytes 12976128 | tf_op jit(solution)/shard_map/all_gather | solution.py:89
  68.1 352.8 %all-gather.21.cloned.1.call-start = ((), (), s32[]{:S(2)}) async-start(), calls=%async_computation.7 | async-start | bytes 2621440 | tf_op jit(solution)/shard_map/all_gather | solution.py:35
  236.6 2.8 copy-start.45
  237.6 2.9 copy-start.49
  237.6 3.1 copy-start.8
  237.6 3.1 copy-start.10
  237.6 3.1 copy-start.47
  239.3 42.3 %copy-start.12 = (f32[8,128,128]{2,1,0:T(8,128)S(1)}, f32[8,128,128]{2,1,0:T(8,128)}, u32[]{:S(2)}) copy-start(f32[8,128,128]{2,1,0:T(8,128)} %param.9) | copy-start | bytes 1572868
  283.4 145.1 %copy-start.38 = (f32[256,8]{0,1:T(8,128)}, f32[256,8]{0,1:T(8,128)S(1)}, u32[]{:S(2)}) copy-start(f32[256,8]{0,1:T(8,128)S(1)} %get-tuple-element.64) | copy-start | bytes 24580
  284.3 144.2 %copy-start.40 = (f32[256,8]{0,1:T(8,128)}, f32[256,8]{0,1:T(8,128)S(1)}, u32[]{:S(2)}) copy-start(f32[256,8]{0,1:T(8,128)S(1)} %get-tuple-element.66) | copy-start | bytes 24580
  284.4 2.8 copy-start.1
  284.4 2.8 copy-start.3
  360.8 21.6 %copy-start.28 = (bf16[256,8,128]{2,0,1:T(8,128)(2,1)S(1)}, bf16[256,8,128]{2,0,1:T(8,128)(2,1)}, u32[]{:S(2)}) copy-start(bf16[256,8,128]{2,0,1:T(8,128)(2,1)} %copy-done.27) | copy-start | bytes 1572868
  360.8 21.6 %copy-start.33 = (f32[8,192,256]{2,1,0:T(8,128)S(1)}, f32[8,192,256]{2,1,0:T(8,128)}, u32[]{:S(2)}) copy-start(f32[8,192,256]{2,1,0:T(8,128)} %get-tuple-element.69) | copy-start | bytes 4718596
  360.8 21.6 %copy-start.34 = (f32[8,128,192]{1,2,0:T(8,128)S(1)}, f32[8,128,192]{1,2,0:T(8,128)}, u32[]{:S(2)}) copy-start(f32[8,128,192]{1,2,0:T(8,128)} %convolution_multiply_fusion.1) | copy-start | bytes 2359300
  382.4 3.7 copy-start.35
  388.6 114.7 %all-gather.17.cloned.1.call-start = ((), (), s32[]{:S(2)}) async-start(), calls=%async_computation.3 | async-start | bytes 4718592 | tf_op jit(solution)/shard_map/all_gather | solution.py:35
  423.4 35.2 %copy-start.2 = (f32[256,8,64]{0,2,1:T(8,128)S(1)}, f32[256,8,64]{0,2,1:T(8,128)}, u32[]{:S(2)}) copy-start(f32[256,8,64]{0,2,1:T(8,128)} %copy-done.1) | copy-start | bytes 1572868
  423.4 159.1 %all-reduce.12.cloned.1.call-start = ((), (), s32[]{:S(2)}) async-start(), calls=%async_computation.4 | async-start | bytes 1048576 | tf_op jit(solution)/shard_map/psum | solution.py:46
  456.6 2.0 copy-start.4
  458.6 1.9 copy-start.6
  460.5 1.8 copy-start.18
  460.6 1.8 copy-start.20
  503.2 4.8 copy-start.14
  503.2 4.8 copy-start.16
  503.9 4.2 copy-start.42
  503.9 4.2 copy-start.43
  508.9 95.7 %copy-start.37 = (bf16[192,8,128]{2,0,1:T(8,128)(2,1)S(1)}, bf16[192,8,128]{2,0,1:T(8,128)(2,1)}, u32[]{:S(2)}) copy-start(bf16[192,8,128]{2,0,1:T(8,128)(2,1)} %get-tuple-element.22) | copy-start | bytes 1179652
  508.9 96.7 %copy-start.36 = (bf16[192,8,128]{2,0,1:T(8,128)(2,1)S(1)}, bf16[192,8,128]{2,0,1:T(8,128)(2,1)}, u32[]{:S(2)}) copy-start(bf16[192,8,128]{2,0,1:T(8,128)(2,1)} %get-tuple-element.25) | copy-start | bytes 1179652
  509.8 121.8 %all-reduce.14.cloned.1.call-start = ((), (), s32[]{:S(2)}) async-start(), calls=%async_computation.5 | async-start | bytes 1048576 | tf_op jit(solution)/shard_map/psum | solution.py:46
  (17 other events, 16.3 us)
Sparse Core Ops, SparseCore 0:
  28.9 35.2 all-gather.18
  66.9 53.5 all-gather.14
  123.7 117.9 all-gather.10
  244.7 116.0 all-gather.12
  388.7 32.1 all-gather.20
  423.5 53.2 all-gather.16
  509.9 72.4 all-reduce.11
  584.8 46.7 all-reduce.13
where the time goes:
time: 648 us; the launch traced here: 641 us
  blocking collectives  293 us (45%)
  waiting for transfers between devices  161 us (25%)
  matrix products  69.6 us (11%)
  between operations  47.3 us (7%)
  other arithmetic  41.7 us (6%)
  local copies, waits for them, and re-layouts  18.9 us (3%)
  starting transfers between devices  10.2 us (2%)
    unnamed x4, blocking collectives  173 us
    psum x2, waiting for transfers between devices, over_axes(): return functools.reduce(lax.psum, axes, array)  97.6 us
    all_gather x4, blocking collectives, carried_in(): pieces = jax.tree.map(lambda part: lax.all_gather(part, axis), subtotal)  76.9 us
    psum x4, blocking collectives, over_axes(): return functools.reduce(lax.psum, axes, array)  42.6 us
    all_gather x4, waiting for transfers between devices, carried_in(): pieces = jax.tree.map(lambda part: lax.all_gather(part, axis), subtotal)  35.9 us
    all_gather x1, waiting for transfers between devices, body(): value_piece = lax.all_gather(values, SEQ, axis=0, tiled=True)  25.6 us
    dot_general x1, matrix products, body(): jnp.einsum('ihj,jhd->ihd', probabilities.astype(jnp.bfloat16), value_piec...  21.6 us
    reduce_sum x1, other arithmetic, body(): totals = jnp.sum(probabilities, axis=-1)  19.2 us
  transfers between devices with their start and end apart: 11, of which 6 were waited for; matrix products, arithmetic and copies ran while one was open for 13% of the time, Pallas kernels for 0%

commit v1 on v0

v1 whole, which is shorter than its diff:
```python
import functools
import math

import jax
import jax.numpy as jnp
from jax import lax
from jax.experimental import pallas as pl
from jax.experimental.pallas import tpu as pltpu
from jax.sharding import Mesh
from jax.sharding import PartitionSpec as P

SEQ = ("seq_0", "seq_1")
MESH = pl.DeviceIdType.MESH

TOKENS=6144; BLK=192; NB=8; WINDOW=64; LOC=384; GRP=768; TK=512
F32=jnp.float32; BF=jnp.bfloat16
NEG=-1e30

def mm(a,b,ca=1,cb=0):
    return lax.dot_general(a,b,(((ca,),(cb,)),((),())),preferred_element_type=F32)

def hilo(a):
    hi=a.astype(BF)
    return hi,(a-hi.astype(F32)).astype(BF)

def local_start(b):
    s=((192*b-64)//128)*128
    return jnp.clip(s,0,TOKENS-LOC)

def compute_kernel(norm, st_ref, q_ref, k_ref, v_ref, w_ref, t_ref, y_ref, dw_ref, loss_ref,
                   vx, pkT, dpT, st_s, ds_s, pq_s, dwq_s):
    st1,st2,st3,xi = st_ref[0],st_ref[1],st_ref[2],st_ref[3]
    def dstart(i):
        return jnp.where(i>=st3,st3,jnp.where(i>=st2,st2,jnp.where(i>=st1,st1,0)))
    scale=128**-0.5
    c2=scale*math.log2(math.e)
    w=w_ref[...]
    half=64
    wq=jnp.concatenate([w[:,:half],-w[:,:half]],axis=1)
    wk=jnp.concatenate([w[:,half:],-w[:,half:]],axis=1)
    wqh,wql=hilo(wq)
    wq2=jnp.concatenate([wqh,wql],axis=1)
    wkh,wkl=hilo(wk.T)

    def kfeat(c,_):
        o=pl.multiple_of(c*GRP,GRP)
        kk=k_ref[pl.ds(o,GRP),:]
        vx[pl.ds(o,GRP),:128]=v_ref[pl.ds(o,GRP),:]
        vx[pl.ds(o,GRP),128:]=jnp.ones((GRP,128),BF)
        l=mm(wkh,kk,1,1)+mm(wkl,kk,1,1)
        for h in (0,half):
            lh=l[h:h+half]
            e=jnp.exp(lh-jnp.max(lh,axis=0,keepdims=True))
            pkT[h:h+half,pl.ds(o,GRP)]=e/jnp.sum(e,axis=0,keepdims=True)
        dpT[:,pl.ds(o,GRP)]=jnp.zeros((128,GRP),F32)
        return 0
    lax.fori_loop(0,TOKENS//GRP,kfeat,0)

    dwq_s[...]=jnp.zeros_like(dwq_s)
    loss_ref[...]=jnp.zeros_like(loss_ref)
    st_s[...]=jnp.zeros_like(st_s)

    def block(z,_):
        b=4*z+xi
        i0=192*b
        ls=pl.multiple_of(local_start(b),128)
        prev=jnp.where(z>0,local_start(b-4),0)
        q=q_ref[z]
        kl=k_ref[pl.ds(ls,LOC),:]
        vl=vx[pl.ds(ls,LOC),:]
        icol=i0+lax.broadcasted_iota(jnp.int32,(BLK,1),0)
        dcol=dstart(icol)
        jrow=ls+lax.broadcasted_iota(jnp.int32,(1,LOC),1)
        same=jrow>=dcol
        s=mm(q,kl,1,1)
        vis=same&(jrow<=icol)
        sm=jnp.where(vis,s,NEG)
        m=jnp.max(sm,axis=1,keepdims=True)
        p=jnp.exp2((sm-m)*c2)
        acc=mm(p.astype(BF),vl)
        lo=dstart(i0)
        def tile(n,carry):
            m,acc=carry
            hi_=ls-n*TK
            ts=pl.multiple_of(jnp.maximum(hi_-TK,0),128)
            kt=k_ref[pl.ds(ts,TK),:]
            vt=vx[pl.ds(ts,TK),:]
            jr=ts+lax.broadcasted_iota(jnp.int32,(1,TK),1)
            sc=mm(q,kt,1,1)
            jr=jnp.where(jr<hi_,jr,-1)
            sc=jnp.where(jr>=dcol,sc,NEG)
            mn=jnp.maximum(m,jnp.max(sc,axis=1,keepdims=True))
            al=jnp.exp2((m-mn)*c2)
            pp=jnp.exp2((sc-mn)*c2)
            acc=acc*al+mm(pp.astype(BF),vt)
            return mn,acc
        ntile=jnp.maximum((ls-lo+TK-1)//TK,0)
        m,acc=lax.fori_loop(0,ntile,tile,(m,acc))
        t=(acc[:,:128]/acc[:,128:]).astype(BF)
        t_ref[z]=t
        lq=mm(q,wq2)
        lq=lq[:,:128]+lq[:,128:]
        ph=[]
        for h in (0,half):
            lh=lq[:,h:h+half]
            e=jnp.exp(lh-jnp.max(lh,axis=1,keepdims=True))
            ph.append(e/jnp.sum(e,axis=1,keepdims=True))
        pq=jnp.concatenate(ph,axis=1)
        pq_h,pq_l=hilo(pq)
        gs=pl.multiple_of(jnp.maximum(ls-GRP,0),128)
        dtag=dstart(ls-1)
        jg=gs+lax.broadcasted_iota(jnp.int32,(1,GRP),1)
        gm=(jg>=jnp.maximum(dtag,prev))&(jg<ls)
        pg=jnp.where(gm,pkT[:,pl.ds(gs,GRP)],0.0).astype(BF)
        keep=jnp.where(dtag<prev,1.0,0.0)
        st=st_s[...]*keep+mm(pg,vx[pl.ds(gs,GRP),:])
        st_s[...]=st
        uses=jnp.where((dcol==dtag)&(ls>0),1.0,0.0)
        sh,sl=hilo(st)
        sth=mm(pq_h,sh)+mm(pq_l,sh)+mm(pq_h,sl)
        inw=same&(jrow<=icol)&(jrow>icol-WINDOW)
        swm=jnp.where(inw,s,NEG)
        mw=jnp.max(swm,axis=1,keepdims=True)
        a=jnp.exp2((swm-mw)*c2)
        bey=same&(jrow<=icol-WINDOW)
        pl_T=pkT[:,pl.ds(ls,LOC)].astype(BF)
        bb=jnp.where(bey,mm(pq_h,pl_T),0.0)
        nd=mm((a+bb).astype(BF),vl)+uses*sth
        rden=1.0/nd[:,128:]
        y=nd[:,:128]*rden
        y_ref[z]=y.astype(BF)
        e=y-t.astype(F32)
        loss_ref[...]+=jnp.sum((e*e).reshape(BLK//8,8,128),axis=0)
        g=e*rden*(2.0*norm)
        gx=jnp.concatenate([g,-g*y],axis=1)
        gh,gl=hilo(gx)
        db=jnp.where(bey,mm(gh,vl,1,1),0.0).astype(BF)
        gu=gx*uses
        guh,gul=hilo(gu)
        dpq=mm(db,pl_T,1,1)+mm(guh,sh,1,1)+mm(gul,sh,1,1)+mm(guh,sl,1,1)
        dpT[:,pl.ds(ls,LOC)]+=mm(pq_h,db,0,0)
        ds_s[z]=mm(pq_h,guh,0,0)
        out=[]
        for h in (0,half):
            pp=pq[:,h:h+half]; dd=dpq[:,h:h+half]
            out.append(pp*(dd-jnp.sum(pp*dd,axis=1,keepdims=True)))
        dl=jnp.concatenate(out,axis=1)
        dh,dlo=hilo(dl)
        dwq_s[...]+=mm(q,jnp.concatenate([dh,dlo],axis=1),0,0)
        return 0
    lax.fori_loop(0,NB,block,0)

    st_s[...]=jnp.zeros_like(st_s)
    def back(n,_):
        z=NB-1-n
        b=4*z+xi
        ls=pl.multiple_of(local_start(b),128)
        prev=jnp.where(z>0,local_start(b-4),0)
        nxt=jnp.where(z<NB-1,local_start(b+4),ls)
        dtag=dstart(ls-1)
        keep=jnp.where(dstart(nxt-1)==dtag,1.0,0.0)
        r=st_s[...]*keep+ds_s[z]
        st_s[...]=r
        gs=pl.multiple_of(jnp.maximum(ls-GRP,0),128)
        jg=gs+lax.broadcasted_iota(jnp.int32,(1,GRP),1)
        gm=(jg>=jnp.maximum(dtag,prev))&(jg<ls)
        d=mm(r.astype(BF),vx[pl.ds(gs,GRP),:],1,1)
        dpT[:,pl.ds(gs,GRP)]+=jnp.where(gm,d,0.0)
        return 0
    lax.fori_loop(0,NB,back,0)

    def fin(c,acc):
        o=pl.multiple_of(c*GRP,GRP)
        out=[]
        for h in (0,half):
            pp=pkT[h:h+half,pl.ds(o,GRP)]; dd=dpT[h:h+half,pl.ds(o,GRP)]
            out.append(pp*(dd-jnp.sum(pp*dd,axis=0,keepdims=True)))
        dl=jnp.concatenate(out,axis=0)
        dh,dlo=hilo(dl)
        kk=k_ref[pl.ds(o,GRP),:]
        return acc+mm(dh,kk)+mm(dlo,kk)
    dk=lax.fori_loop(0,TOKENS//GRP,fin,jnp.zeros((128,128),F32))
    dkt=dk.T
    dq=dwq_s[:,:128]+dwq_s[:,128:]
    dw_ref[...]=jnp.concatenate([dq[:,:half]-dq[:,half:],dkt[:,:half]-dkt[:,half:]],axis=1)

def compute(norm, st, q, k, v, w):
    V=pl.BlockSpec(memory_space=pltpu.VMEM)
    return pl.pallas_call(
        functools.partial(compute_kernel,norm),
        out_shape=(jax.ShapeDtypeStruct((NB,BLK,128),BF),jax.ShapeDtypeStruct((NB,BLK,128),BF),
                   jax.ShapeDtypeStruct((128,128),F32),jax.ShapeDtypeStruct((8,128),F32)),
        in_specs=[pl.BlockSpec(memory_space=pltpu.SMEM)]+[V]*4,
        out_specs=(V,)*4,
        scratch_shapes=[pltpu.VMEM((TOKENS,256),BF),pltpu.VMEM((128,TOKENS),F32),pltpu.VMEM((128,TOKENS),F32),
                        pltpu.VMEM((128,256),F32),pltpu.VMEM((NB,128,256),F32),pltpu.VMEM((BLK,128),F32),pltpu.VMEM((128,256),F32)],
        compiler_params=pltpu.CompilerParams(vmem_limit_bytes=60<<20),
    )(st,q,k,v,w)


NZ, NX = 8, 4
ORDER = (0, 1, 7, 2, 6, 3, 5, 4)


def rcopy(src, dst, ssem, rsem, **where):
    return pltpu.make_async_remote_copy(
        src_ref=src, dst_ref=dst, send_sem=ssem, recv_sem=rsem,
        device_id=where, device_id_type=MESH)


def greet(peers):
    barrier = pltpu.get_barrier_semaphore()
    for peer in peers:
        pl.semaphore_signal(barrier, inc=1, device_id=peer, device_id_type=MESH)
    pl.semaphore_wait(barrier, len(peers))


def gather_kernel(q_ref, k_ref, v_ref, c_ref, qa, ka, va, ca,
                  zs, zr, rs, rr, ls, lr, ys, yr, cs, cr, own):
    z, x = lax.axis_index("seq_0"), lax.axis_index("seq_1")
    right, left = lax.rem(x + 1, NX), lax.rem(x + 3, NX)
    greet([{"seq_0": lax.rem(z + d, NZ)} for d in range(1, NZ)]
          + [{"seq_1": lax.rem(x + d, NX)} for d in range(1, NX)])
    me = NX * z + x
    local = [pltpu.make_async_copy(k_ref.at[z], ka.at[me], own.at[0]),
             pltpu.make_async_copy(v_ref.at[z], va.at[me], own.at[1]),
             pltpu.make_async_copy(q_ref.at[z], qa.at[z], own.at[2]),
             pltpu.make_async_copy(c_ref, ca.at[x, z], own.at[3])]
    for c in local:
        c.start()
    sent = []
    for ref, dst, i in ((k_ref, ka, 0), (v_ref, va, 1), (q_ref, qa, 2)):
        for d in ORDER[1:]:
            t = lax.rem(z + d, NZ)
            c = rcopy(ref.at[t], dst.at[z if i == 2 else me], zs.at[i, t], zr.at[i, z], seq_0=t)
            c.start()
            sent.append(c)
        if i == 0:
            for d in ORDER[1:]:
                t = lax.rem(z + d, NZ)
                c = rcopy(c_ref, ca.at[x, z], zs.at[3, t], zr.at[3, z], seq_0=t)
                c.start()
                sent.append(c)

    def arrived(i, s, dst):
        rcopy(dst, dst, zs.at[i, s], zr.at[i, s], seq_0=s).wait_recv()

    for c in local:
        c.wait()
    relayed = []

    def relay(s):
        slot = NX * s + left
        c = rcopy(ka.at[slot], ka.at[slot], rs.at[0, s], rr.at[0, s], seq_1=right)
        c.wait_recv()
        c = rcopy(ka.at[slot], ka.at[slot], ys.at[0, s], yr.at[0, s], seq_1=right)
        c.start()
        relayed.append(c)
        slot = NX * s + right
        c = rcopy(va.at[slot], va.at[slot], ls.at[1, s], lr.at[1, s], seq_1=left)
        c.wait_recv()
        c = rcopy(va.at[slot], va.at[slot], ys.at[1, s], yr.at[1, s], seq_1=left)
        c.start()
        relayed.append(c)

    last = None
    for d in ORDER:
        s = lax.rem(z + d, NZ)
        slot = NX * s + x
        for i, arr in ((0, ka), (1, va)):
            if d:
                arrived(i, s, arr.at[slot])
            for sems, semr, to in ((rs, rr, right), (ls, lr, left)):
                c = rcopy(arr.at[slot], arr.at[slot], sems.at[i, s], semr.at[i, s], seq_1=to)
                c.start()
                sent.append(c)
        if last is not None:
            relay(last)
        last = s
    for d in ORDER[1:]:
        s = lax.rem(z + d, NZ)
        arrived(3, s, ca.at[x, s])
    for d in range(1, NX):
        t = lax.rem(x + d, NX)
        c = rcopy(ca.at[x], ca.at[x], cs.at[t], cr.at[x], seq_1=t)
        c.start()
        sent.append(c)
    relay(last)
    for d in ORDER[1:]:
        s = lax.rem(z + d, NZ)
        arrived(2, s, qa.at[s])
    for d in range(1, NX):
        s = lax.rem(x + d, NX)
        rcopy(ca.at[s], ca.at[s], cs.at[s], cr.at[s], seq_1=s).wait_recv()
    far = lax.rem(x + 2, NX)
    for d in ORDER:
        s = lax.rem(z + d, NZ)
        slot = NX * s + left
        rcopy(va.at[slot], va.at[slot], rs.at[1, s], rr.at[1, s], seq_1=right).wait_recv()
        slot = NX * s + right
        rcopy(ka.at[slot], ka.at[slot], ls.at[0, s], lr.at[0, s], seq_1=left).wait_recv()
        slot = NX * s + far
        rcopy(ka.at[slot], ka.at[slot], ys.at[0, s], yr.at[0, s], seq_1=right).wait_recv()
        rcopy(va.at[slot], va.at[slot], ys.at[1, s], yr.at[1, s], seq_1=left).wait_recv()
    for c in sent + relayed:
        c.wait_send()


def gather(q, k, v, counts):
    A = pl.BlockSpec(memory_space=pl.ANY)
    D = pltpu.SemaphoreType.DMA
    return pl.pallas_call(
        gather_kernel,
        out_shape=(jax.ShapeDtypeStruct((NZ, BLK, 128), BF),
                   jax.ShapeDtypeStruct((NZ * NX, BLK, 128), BF),
                   jax.ShapeDtypeStruct((NZ * NX, BLK, 128), BF),
                   jax.ShapeDtypeStruct((NX, NZ, 8, 128), F32)),
        in_specs=[A] * 4, out_specs=(A,) * 4,
        scratch_shapes=[D((4, NZ)), D((4, NZ)), D((2, NZ)), D((2, NZ)), D((2, NZ)), D((2, NZ)),
                        D((2, NZ)), D((2, NZ)), D((NX,)), D((NX,)), D((4,))],
        compiler_params=pltpu.CompilerParams(collective_id=0, has_side_effects=True),
    )(q, k, v, counts)


def spread_kernel(t_ref, y_ref, dw_ref, l_ref, ta, ya, wa, la,
                  wx, wsum, lx, lz, lc, fin,
                  zs, zr, xs, xr, gs, gr, own):
    z, x = lax.axis_index("seq_0"), lax.axis_index("seq_1")
    h, g = lax.axis_index("head"), lax.axis_index("grp")
    cols = [{"grp": lax.rem(g + (d // NX), 2), "head": lax.rem(h + d % NX, NX)} for d in range(1, 8)]
    greet([{"seq_0": lax.rem(z + d, NZ)} for d in range(1, NZ)]
          + [{"seq_1": lax.rem(x + d, NX)} for d in range(1, NX)] + cols)
    local = [pltpu.make_async_copy(t_ref.at[z], ta.at[z], own.at[0]),
             pltpu.make_async_copy(y_ref.at[z], ya.at[z], own.at[1]),
             pltpu.make_async_copy(dw_ref, wx.at[x], own.at[2]),
             pltpu.make_async_copy(l_ref, lx.at[x], own.at[3])]
    for c in local:
        c.start()
    sent = []
    for i, (src, dst) in enumerate(((dw_ref, wx), (l_ref, lx))):
        for d in range(1, NX):
            t = lax.rem(x + d, NX)
            c = rcopy(src, dst.at[x], xs.at[i, t], xr.at[i, x], seq_1=t)
            c.start()
            sent.append(c)
    for i, (src, dst) in enumerate(((t_ref, ta), (y_ref, ya))):
        for d in ORDER[1:]:
            t = lax.rem(z + d, NZ)
            c = rcopy(src.at[t], dst.at[z], zs.at[i, t], zr.at[i, z], seq_0=t)
            c.start()
            sent.append(c)
    for c in local:
        c.wait()
    for i, dst in enumerate((wx, lx)):
        for d in range(1, NX):
            s = lax.rem(x + d, NX)
            rcopy(dst.at[s], dst.at[s], xs.at[i, s], xr.at[i, s], seq_1=s).wait_recv()
    wsum[...] = (wx[0] + wx[1]) + (wx[2] + wx[3])
    lz[z] = (lx[0] + lx[1]) + (lx[2] + lx[3])
    keep = pltpu.make_async_copy(wsum, wa.at[z], own.at[2])
    keep.start()
    for d in ORDER[1:]:
        t = lax.rem(z + d, NZ)
        c = rcopy(lz.at[z], lz.at[z], zs.at[3, t], zr.at[3, z], seq_0=t)
        c.start()
        sent.append(c)
        c = rcopy(wsum, wa.at[z], zs.at[2, t], zr.at[2, z], seq_0=t)
        c.start()
        sent.append(c)
    for d in ORDER[1:]:
        s = lax.rem(z + d, NZ)
        rcopy(lz.at[s], lz.at[s], zs.at[3, s], zr.at[3, s], seq_0=s).wait_recv()
    part = lz[0]
    for i in range(1, NZ):
        part = part + lz[i]
    mine = NX * g + h
    lc[mine] = part
    for d, peer in zip(range(1, 8), cols):
        there = NX * peer["grp"] + peer["head"]
        c = rcopy(lc.at[mine], lc.at[mine], gs.at[there], gr.at[mine], **peer)
        c.start()
        sent.append(c)
    for peer in cols:
        there = NX * peer["grp"] + peer["head"]
        rcopy(lc.at[there], lc.at[there], gs.at[there], gr.at[there], **peer).wait_recv()
    part = lc[0]
    for i in range(1, 8):
        part = part + lc[i]
    total = jnp.sum(jnp.sum(part, axis=0, keepdims=True), axis=1, keepdims=True)
    fin[...] = jnp.broadcast_to(total, (8, 128))
    done = pltpu.make_async_copy(fin, la, own.at[3])
    done.start()
    for d in ORDER[1:]:
        s = lax.rem(z + d, NZ)
        for i, dst in enumerate((ta, ya, wa)):
            rcopy(dst.at[s], dst.at[s], zs.at[i, s], zr.at[i, s], seq_0=s).wait_recv()
    for c in sent:
        c.wait_send()
    keep.wait()
    done.wait()


def spread(t, y, dw, l):
    A = pl.BlockSpec(memory_space=pl.ANY)
    D = pltpu.SemaphoreType.DMA
    V = pltpu.VMEM
    return pl.pallas_call(
        spread_kernel,
        out_shape=(jax.ShapeDtypeStruct((NZ, BLK, 128), BF),
                   jax.ShapeDtypeStruct((NZ, BLK, 128), BF),
                   jax.ShapeDtypeStruct((NZ, 128, 128), F32),
                   jax.ShapeDtypeStruct((8, 128), F32)),
        in_specs=[A] * 4, out_specs=(A,) * 4,
        scratch_shapes=[V((NX, 128, 128), F32), V((128, 128), F32), V((NX, 8, 128), F32),
                        V((NZ, 8, 128), F32), V((8, 8, 128), F32), V((8, 128), F32),
                        D((4, NZ)), D((4, NZ)), D((2, NX)), D((2, NX)), D((8,)), D((8,)), D((4,))],
        compiler_params=pltpu.CompilerParams(collective_id=1, has_side_effects=True),
    )(t, y, dw, l)


def body(queries, keys, values, documents, feature_map):
    z, x = lax.axis_index("seq_0"), lax.axis_index("seq_1")
    norm = 1.0 / (TOKENS * 64)
    below = [jnp.sum((documents < d).astype(F32)) for d in (1, 2, 3)]
    row = jnp.stack(below + [jnp.float32(0)] * 5)
    counts = jnp.broadcast_to(row[:, None], (8, 128))
    turned = [jnp.swapaxes(a, 0, 1) for a in (queries, keys, values)]
    qa, ka, va, ca = gather(*turned, counts)
    starts = jnp.sum(ca[:, :, :, 0], axis=(0, 1)).astype(jnp.int32)
    scalars = jnp.concatenate([starts[:3], jnp.stack([x, z]).astype(jnp.int32)])
    w = lax.dynamic_index_in_dim(feature_map, z, 0, keepdims=False)
    t, y, dw, loss = compute(norm, scalars, qa, ka.reshape(TOKENS, 128), va.reshape(TOKENS, 128), w)
    ta, ya, wa, la = spread(t, y, dw, loss * norm)
    return (jnp.swapaxes(ta, 0, 1), jnp.swapaxes(ya, 0, 1), la[0, 0], wa)


def solution(mesh):
    split = Mesh(
        mesh.devices.reshape(mesh.shape["grp"], 8, 4, mesh.shape["head"]),
        ("grp", "seq_0", "seq_1", "head"),
    )
    return jax.shard_map(
        body,
        mesh=split,
        in_specs=(
            P(SEQ, ("grp", "head"), None),
            P(SEQ, ("grp", "head"), None),
            P(SEQ, ("grp", "head"), None),
            P(SEQ),
            P(("grp", "head"), None, None),
        ),
        out_specs=(
            P(SEQ, ("grp", "head"), None),
            P(SEQ, ("grp", "head"), None),
            P(),
            P(("grp", "head"), None, None),
        ),
        check_vma=False,
    )
```

time: 648 us -> 152 us (0.23)
  the two profiles are of different devices: /device:TPU:32 before, /device:TPU:7 now
where the time goes in v1:
time: 152 us; the launch traced here: 153 us
  Pallas kernels  135 us (89%)
  local copies, waits for them, and re-layouts  12.3 us (8%)
  other arithmetic  4.35 us (3%)
    pallas_call x1, Pallas kernels, compute(): pl.pallas_call(functools.partial(compute_kernel, norm), out_shape=(jax.Sh...  48.7 us
    pallas_call x1, Pallas kernels, spread(): pl.pallas_call(spread_kernel, out_shape=(jax.ShapeDtypeStruct((NZ, BLK, 1...  45.4 us
    pallas_call x1, Pallas kernels, gather(): pl.pallas_call(gather_kernel, out_shape=(jax.ShapeDtypeStruct((NZ, BLK, 1...  41.1 us
    unnamed x10, local copies, waits for them, and re-layouts  5.68 us

profile of v1, /device:TPU:7, one launch (start us, length us, event | category | flops | bytes accessed | tf_op | source)
XLA Modules:
  0.0 152.6 jit_solution(13581488908256358482)
XLA Ops:
  0.6 0.0 copy-start
  0.6 0.0 copy-start.2
  0.7 1.4 fusion.2
  2.0 2.0 %stack.21 = f32[8]{0:T(128)S(1)} concatenate(f32[1]{0:T(128)} %bitcast.3, f32[1]{0:T(128)} %bitcast.4, f32[1]{0:T(128)} %bitcast.5, f32[1]{0:T(128)} %constant.10.clone.1, f32[4]{0:T(128)S(1)} %broadcast.4), dimensions={0} | concatenate | bytes 64 | tf_op jit(solution)/shard_map/stack | solution.py:425
  4.1 0.7 broadcast_in_dim.2.c_ref
  4.7 2.1 %copy_bitcast_fusion = (bf16[8,192,128]{2,1,0:T(8,128)(2,1)}, bf16[8,192,128]{2,1,0:T(8,128)(2,1)}) fusion(bf16[192,8,128]{2,1,0:T(8,128)(2,1)} %param.7, bf16[192,8,128]{2,1,0:T(8,128)(2,1)} %param.6), kind=kLoop, calls=%fused_computation | loop fusion | bytes 1572864 | tf_op jit(solution)/shard_map/transpose | solution.py:427
  6.8 0.0 copy-done.2
  6.8 0.8 copy.17
  7.7 41.1 %shard_map.84 = (bf16[8,192,128]{2,1,0:T(8,128)(2,1)}, bf16[32,192,128]{2,1,0:T(8,128)(2,1)}, bf16[32,192,128]{2,1,0:T(8,128)(2,1)}, f32[4,8,8,128]{3,2,1,0:T(8,128)}) custom-call(bf16[8,192,128]{2,1,0:T(8,128)(2,1)} %bitcast.20, bf16[8,192,128]{2,1,0:T(8,128)(2,1)} %get-tuple-element.36.k_ref, bf16[8,192,128]{2,1,0:T(8,128)(2,1)} %get-tuple-element.35.v_ref, ...), custom_call_target="tpu_custom_call" | custom-call | tf_op jit(solution)/shard_map/pallas_call | solution.py:312
  48.8 1.1 slice_reduce_fusion
  49.9 0.7 pad_add_fusion.st_ref
  50.5 0.0 copy-done
  50.5 0.6 dynamic-slice_bitcast_fusion.w_ref
  51.2 48.7 %shard_map.85 = (bf16[8,192,128]{2,1,0:T(8,128)(2,1)}, bf16[8,192,128]{2,1,0:T(8,128)(2,1)}, f32[128,128]{1,0:T(8,128)}, f32[8,128]{1,0:T(8,128)}) custom-call(s32[5]{0:T(128)} %pad_add_fusion.st_ref, bf16[8,192,128]{2,1,0:T(8,128)(2,1)} %get-tuple-element.17.q_ref, bf16[6144,128]{1,0:T(8,128)(2,1)} %bitcast.21, bf16[6144,128]{1,0:T(8,128)(2,1)} %bitcast.22, ...), custom_call_target="tpu_custom_call" | custom-call | tf_op jit(solution)/shard_map/pallas_call | solution.py:189
  99.9 1.3 broadcast_multiply_fusion.l_ref
  101.1 45.4 %shard_map.86 = (bf16[8,192,128]{2,1,0:T(8,128)(2,1)}, bf16[8,192,128]{2,1,0:T(8,128)(2,1)}, f32[8,128,128]{2,1,0:T(8,128)}, f32[8,128]{1,0:T(8,128)}) custom-call(bf16[8,192,128]{2,1,0:T(8,128)(2,1)} %get-tuple-element.20.t_ref, bf16[8,192,128]{2,1,0:T(8,128)(2,1)} %get-tuple-element.21.y_ref, f32[128,128]{1,0:T(8,128)} %get-tuple-element.22.dw_ref, ...), custom_call_target="tpu_custom_call" | custom-call | tf_op jit(solution)/shard_map/pallas_call | solution.py:407
  146.6 0.0 copy-start.1
  146.6 2.1 %copy.12 = bf16[192,8,128]{2,1,0:T(8,128)(2,1)} copy(bf16[192,8,128]{2,0,1:T(8,128)(2,1)} %bitcast.24) | data formatting | bytes 786432
  148.6 2.0 %copy.13 = bf16[192,8,128]{2,1,0:T(8,128)(2,1)} copy(bf16[192,8,128]{2,0,1:T(8,128)(2,1)} %bitcast.23) | data formatting | bytes 786432
  150.6 1.2 slice.11
  151.8 0.0 copy-done.1
  151.8 0.8 copy.19
  (2 shorter events, 0.0 us)
Async XLA Ops:
  0.6 49.9 %copy-start = (f32[8,128,128]{2,1,0:T(8,128)S(1)}, f32[8,128,128]{2,1,0:T(8,128)}, u32[]{:S(2)}) copy-start(f32[8,128,128]{2,1,0:T(8,128)} %param.9) | copy-start | bytes 1572868
  0.6 6.2 %copy-start.2 = (bf16[192,8,128]{2,1,0:T(8,128)(2,1)S(1)}, bf16[192,8,128]{2,1,0:T(8,128)(2,1)}, u32[]{:S(2)}) copy-start(bf16[192,8,128]{2,1,0:T(8,128)(2,1)} %param.5) | copy-start | bytes 1179652
  146.6 5.3 %copy-start.1 = (f32[8,128,128]{2,1,0:T(8,128)S(1)}, f32[8,128,128]{2,1,0:T(8,128)}, u32[]{:S(2)}) copy-start(f32[8,128,128]{2,1,0:T(8,128)} %get-tuple-element.44) | copy-start | bytes 1572868

commit v2 on v0

v2 whole, which is shorter than its diff:
```python
import functools
import math

import jax
import jax.numpy as jnp
from jax import lax
from jax.experimental import pallas as pl
from jax.experimental.pallas import tpu as pltpu
from jax.sharding import Mesh
from jax.sharding import PartitionSpec as P

SEQ = ("seq_0", "seq_1")
MESH = pl.DeviceIdType.MESH

TOKENS, BLK, WINDOW, LOC, GRP, HALF = 6144, 192, 64, 384, 768, 64
NZ, NX = 8, 4
FRONT = 896
ROWS = FRONT + TOKENS + 128
F32, BF = jnp.float32, jnp.bfloat16
NEG = -1e30
SCALE = 128**-0.5
C2 = SCALE * math.log2(math.e)


def mm(a, b, ca=1, cb=0):
    return lax.dot_general(a, b, (((ca,), (cb,)), ((), ())), preferred_element_type=F32)


def hilo(a):
    hi = a.astype(BF)
    return hi, (a - hi.astype(F32)).astype(BF)


def rcopy(src, dst, ssem, rsem, **where):
    return pltpu.make_async_remote_copy(
        src_ref=src, dst_ref=dst, send_sem=ssem, recv_sem=rsem,
        device_id=where, device_id_type=MESH)


def greet(peers):
    barrier = pltpu.get_barrier_semaphore()
    for peer in peers:
        pl.semaphore_signal(barrier, inc=1, device_id=peer, device_id_type=MESH)
    pl.semaphore_wait(barrier, len(peers))


def nth(j):
    odd = lax.rem(j, 2)
    return lax.rem(odd * ((j + 1) // 2) + (1 - odd) * (NZ - j // 2), NZ)


def with_ones(v):
    return jnp.concatenate([v, jnp.ones_like(v)], axis=1)


def iota(shape, dim):
    return lax.broadcasted_iota(jnp.int32, shape, dim).astype(F32)


def kernel(norm, q_ref, k_ref, v_ref, doc_ref, fm_ref, ta, ya, wout, lout,
           qa, ka, va, ca, qe, ke, wq2, wk2, pkT, dpT, ms, accs, tb, yb, sts, dss, run, dwq, pls,
           dwb, wx, wg, lx, lz, lc,
           own, zs, zr, rs, rr, ls_, lr, ys, yr, cs, cr, xs, xr, gs, gr, os, orr):
    z, x = lax.axis_index("seq_0"), lax.axis_index("seq_1")
    h, g = lax.axis_index("head"), lax.axis_index("grp")
    right, left, far = lax.rem(x + 1, NX), lax.rem(x + 3, NX), lax.rem(x + 2, NX)
    cols = [{"grp": lax.rem(g + (d // NX), 2), "head": lax.rem(h + d % NX, NX)} for d in range(1, 8)]

    docs = doc_ref[...]
    row = lax.broadcasted_iota(jnp.int32, (8, 128), 0)
    tile = jnp.zeros((8, 128), F32)
    for d in (1, 2, 3):
        n = jnp.sum((docs < d).astype(F32), axis=1, keepdims=True)
        tile = tile + jnp.where(row == d, jnp.broadcast_to(n, (8, 128)), 0.0)
    ca[x, z] = tile
    zero = jnp.zeros((FRONT, 128), BF)
    ka[:FRONT] = zero
    va[:FRONT] = zero
    ka[FRONT + TOKENS:] = zero[:128]
    va[FRONT + TOKENS:] = zero[:128]
    pkT[:, :FRONT] = jnp.zeros((128, FRONT), F32)
    pkT[:, FRONT + TOKENS:] = jnp.zeros((128, 128), F32)
    w = fm_ref[z]
    wqh, wql = hilo(jnp.concatenate([w[:, :HALF], -w[:, :HALF]], axis=1))
    wq2[...] = jnp.concatenate([wqh, wql], axis=1)
    wkh, wkl = hilo(jnp.concatenate([w[:, HALF:], -w[:, HALF:]], axis=1).T)
    wk2[0] = wkh
    wk2[1] = wkl

    greet([{"seq_0": lax.rem(z + d, NZ)} for d in range(1, NZ)]
          + [{"seq_1": lax.rem(x + d, NX)} for d in range(1, NX)] + cols)

    def krows(arr, s, col):
        return arr.at[pl.ds(pl.multiple_of(FRONT + GRP * s + BLK * col, 64), BLK)]

    def zcopy(i, t):
        src = (k_ref, v_ref, q_ref)[i].at[t]
        dst = qa.at[z] if i == 2 else krows((ka, va)[i], z, x)
        return rcopy(src, dst, zs.at[i, t], zr.at[i, z], seq_0=t)

    def zarrive(i, s):
        dst = qa.at[s] if i == 2 else krows((ka, va)[i], s, x)
        rcopy(dst, dst, zs.at[i, s], zr.at[i, s], seq_0=s).wait_recv()

    def count_copy(t):
        return rcopy(ca.at[x, z], ca.at[x, z], zs.at[3, t], zr.at[3, z], seq_0=t)

    def xcopy(i, s, col, to, sems, semr):
        ref = krows((ka, va)[i], s, col)
        return rcopy(ref, ref, sems.at[i, s], semr.at[i, s], seq_1=to)

    local = [pltpu.make_async_copy(k_ref.at[z], krows(ka, z, x), own.at[0]),
             pltpu.make_async_copy(v_ref.at[z], krows(va, z, x), own.at[1]),
             pltpu.make_async_copy(q_ref.at[z], qa.at[z], own.at[2])]
    for c in local:
        c.start()
    for j in range(1, NZ):
        count_copy(lax.rem(z + nth(j), NZ)).start()

    def send_all(j, _):
        t = lax.rem(z + NZ - nth(j), NZ)
        for i in range(3):
            zcopy(i, t).start()
        return 0
    lax.fori_loop(1, NZ, send_all, 0)
    for c in local:
        c.wait()

    def forward(s):
        for i in range(2):
            xcopy(i, s, x, right, rs, rr).start()
            xcopy(i, s, x, left, ls_, lr).start()

    def relay(s):
        xcopy(0, s, left, right, rs, rr).wait_recv()
        xcopy(0, s, left, right, ys, yr).start()
        xcopy(1, s, right, left, ls_, lr).wait_recv()
        xcopy(1, s, right, left, ys, yr).start()

    def complete(s):
        xcopy(1, s, left, right, rs, rr).wait_recv()
        xcopy(0, s, right, left, ls_, lr).wait_recv()
        xcopy(0, s, far, right, ys, yr).wait_recv()
        xcopy(1, s, far, left, ys, yr).wait_recv()

    forward(z)
    for j in range(1, NZ):
        s = lax.rem(z + j, NZ)
        rcopy(ca.at[x, s], ca.at[x, s], zs.at[3, s], zr.at[3, s], seq_0=s).wait_recv()
    for d in range(1, NX):
        t = lax.rem(x + d, NX)
        rcopy(ca.at[x], ca.at[x], cs.at[t], cr.at[x], seq_1=t).start()
    relay(z)
    for d in range(1, NX):
        s = lax.rem(x + d, NX)
        rcopy(ca.at[s], ca.at[s], cs.at[s], cr.at[s], seq_1=s).wait_recv()
    for d in range(1, NX):
        t = lax.rem(x + d, NX)
        rcopy(ca.at[x], ca.at[x], cs.at[t], cr.at[x], seq_1=t).wait_send()
    tally = jnp.zeros((8, 128), F32)
    for i in range(NX):
        for j in range(NZ):
            tally = tally + ca[i, j]
    st1, st2, st3 = tally[1:2, :1], tally[2:3, :1], tally[3:4, :1]
    lane = lax.broadcasted_iota(jnp.int32, (1, 128), 1)
    full = lambda d: tally[d:d + 1, :]
    low = jnp.where(lane == 0, 0.0, jnp.where(lane == 1, full(1), jnp.where(
        lane == 2, full(2), jnp.where(lane == 3, full(3), 1e9))))
    high = jnp.where(lane == 0, full(1), jnp.where(lane == 1, full(2), jnp.where(
        lane == 2, full(3), 1e9)))

    def dstart(i):
        return jnp.where(i >= st3, st3, jnp.where(i >= st2, st2, jnp.where(i >= st1, st1, 0.0)))

    def qpos(s):
        return (GRP * s + BLK * x).astype(F32) + iota((BLK, 1), 0)

    def absorb(n):
        a = lax.rem(z + nth(n), NZ)
        o = pl.multiple_of(FRONT + GRP * a, 128)
        kk = ka[pl.ds(o, GRP), :]
        l = mm(wk2[0], kk, 1, 1) + mm(wk2[1], kk, 1, 1)
        for f in (0, HALF):
            lh = l[f:f + HALF]
            e = jnp.exp(lh - jnp.max(lh, axis=0, keepdims=True))
            pkT[f:f + HALF, pl.ds(o, GRP)] = e * (1.0 / jnp.sum(e, axis=0, keepdims=True))
        kpos = (GRP * a).astype(F32) + iota((GRP, 1), 0)
        ke[pl.ds(o, GRP), :] = jnp.where((kpos >= low) & (kpos < high), 1.0, 0.0).astype(BF)
        icol = qpos(a)
        miss = jnp.logical_not((icol >= low) & (icol < high)) & (lane < 4)
        qe[a] = jnp.where(miss, NEG, 0.0).astype(BF)
        jrow = (GRP * a).astype(F32) + iota((1, GRP), 1)
        s = mm(qa[a], kk, 1, 1)
        s = jnp.where((jrow <= icol) & (jrow >= dstart(icol)), s, NEG)
        m = jnp.max(s, axis=1, keepdims=True)
        p = jnp.exp2((s - m) * C2)
        ms[a] = m
        accs[a] = mm(p.astype(BF), with_ones(va[pl.ds(o, GRP), :]))

        def pair(j, _):
            b = lax.rem(z + nth(j), NZ)
            ge = (a - b + NZ) // NZ
            zq, zk = ge * a + (1 - ge) * b, ge * b + (1 - ge) * a
            r = pl.multiple_of(FRONT + GRP * zk, 128)
            sc = mm(jnp.concatenate([qa[zq], qe[zq]], axis=1),
                    jnp.concatenate([ka[pl.ds(r, GRP), :], ke[pl.ds(r, GRP), :]], axis=1), 1, 1)
            mo = ms[zq]
            mn = jnp.maximum(mo, jnp.max(sc, axis=1, keepdims=True))
            pp = jnp.exp2((sc - mn) * C2)
            ms[zq] = mn
            accs[zq] = accs[zq] * jnp.exp2((mo - mn) * C2) + mm(
                pp.astype(BF), with_ones(va[pl.ds(r, GRP), :]))
            return 0
        lax.fori_loop(0, n, pair, 0)

    def step(n, _):
        s = lax.rem(z + nth(n), NZ)
        zarrive(0, s)
        zarrive(1, s)
        forward(s)
        prior = lax.rem(z + nth(n - 1), NZ)
        complete(prior)
        absorb(n - 1)
        relay(s)
        zarrive(2, s)
        return 0
    lax.fori_loop(1, NZ, step, 0)
    complete(lax.rem(z + nth(NZ - 1), NZ))
    absorb(jnp.int32(NZ - 1))

    off = BLK * x + 64 * lax.rem(x, 2)
    run[...] = jnp.zeros_like(run)

    def local_row(s):
        return pl.multiple_of(GRP * s + off + GRP, 128)

    def group_mask(s):
        end = (GRP * s + off + GRP - FRONT).astype(F32)
        jg = end - GRP + iota((1, GRP), 1)
        tag = dstart(jnp.zeros((1, 1), F32) + (end - 1.0))
        return (jg >= tag) & (jg < end) & (jg >= 0.0), tag, end

    def states(s, _):
        r = local_row(s)
        mask, tag, end = group_mask(s)
        o = pl.multiple_of(r - GRP, 128)
        pg = jnp.where(mask, pkT[:, pl.ds(o, GRP)], 0.0).astype(BF)
        keep = jnp.where(tag < end - GRP, 1.0, 0.0)
        st = run[...] * keep + mm(pg, with_ones(va[pl.ds(o, GRP), :]))
        run[...] = st
        hi, lo = hilo(st)
        sts[s, 0] = hi
        sts[s, 1] = lo
        tb[s] = (accs[s][:, :128] / accs[s][:, 128:]).astype(BF)
        return 0
    lax.fori_loop(0, NZ, states, 0)

    dwq[...] = jnp.zeros_like(dwq)
    pls[...] = jnp.zeros_like(pls)
    dpT[...] = jnp.zeros_like(dpT)

    def send_out(i, t):
        src, dst = ((tb, ta), (yb, ya))[i]
        return rcopy(src.at[t], dst.at[z], os.at[i, t], orr.at[i, z], seq_0=t)

    def block(n, _):
        s = lax.rem(z + nth(NZ - 1 - n), NZ)

        @pl.when(n < NZ - 1)
        def _():
            send_out(0, s).start()

        @pl.when(n > 0)
        def _():
            send_out(1, lax.rem(z + nth(NZ - n), NZ)).start()
        r = local_row(s)
        q = qa[s]
        kl = ka[pl.ds(r, LOC), :]
        vl = with_ones(va[pl.ds(r, LOC), :])
        icol = qpos(s)
        dcol = dstart(icol)
        jrow = (GRP * s + off + GRP - FRONT).astype(F32) + iota((1, LOC), 1)
        same = jrow >= dcol
        sc = mm(q, kl, 1, 1)
        lq = mm(q, wq2[...])
        lq = lq[:, :128] + lq[:, 128:]
        ph = []
        for f in (0, HALF):
            lh = lq[:, f:f + HALF]
            e = jnp.exp(lh - jnp.max(lh, axis=1, keepdims=True))
            ph.append(e * (1.0 / jnp.sum(e, axis=1, keepdims=True)))
        pq = jnp.concatenate(ph, axis=1)
        pq_h, pq_l = hilo(pq)
        _, tag, end = group_mask(s)
        uses = jnp.where((dcol == tag) & (end > 0.0), 1.0, 0.0)
        sh, sl = sts[s, 0], sts[s, 1]
        sth = mm(pq_h, sh) + mm(pq_l, sh) + mm(pq_h, sl)
        swm = jnp.where(same & (jrow <= icol) & (jrow > icol - WINDOW), sc, NEG)
        a = jnp.exp2((swm - jnp.max(swm, axis=1, keepdims=True)) * C2)
        bey = same & (jrow <= icol - WINDOW)
        pl_T = pkT[:, pl.ds(r, LOC)].astype(BF)
        bb = jnp.where(bey, mm(pq_h, pl_T), 0.0)
        nd = mm((a + bb).astype(BF), vl) + uses * sth
        rden = 1.0 / nd[:, 128:]
        y = nd[:, :128] * rden
        yb[s] = y.astype(BF)
        e = y - tb[s].astype(F32)
        pls[...] += jnp.sum((e * e).reshape(BLK // 8, 8, 128), axis=0)
        gr_ = e * rden * (2.0 * norm)
        gx = jnp.concatenate([gr_, -gr_ * y], axis=1)
        gh, _ = hilo(gx)
        db = jnp.where(bey, mm(gh, vl, 1, 1), 0.0).astype(BF)
        guh, gul = hilo(gx * uses)
        dpq = mm(db, pl_T, 1, 1) + mm(guh, sh, 1, 1) + mm(gul, sh, 1, 1) + mm(guh, sl, 1, 1)
        dpT[:, pl.ds(r, LOC)] += mm(pq_h, db, 0, 0)
        dss[s] = mm(pq_h, guh, 0, 0)
        out = []
        for f in (0, HALF):
            pp, dd = pq[:, f:f + HALF], dpq[:, f:f + HALF]
            out.append(pp * (dd - jnp.sum(pp * dd, axis=1, keepdims=True)))
        dh, dlo = hilo(jnp.concatenate(out, axis=1))
        dwq[...] += mm(q, jnp.concatenate([dh, dlo], axis=1), 0, 0)
        return 0
    lax.fori_loop(0, NZ, block, 0)

    run[...] = jnp.zeros_like(run)

    def back(n, _):
        s = NZ - 1 - n
        o = pl.multiple_of(local_row(s) - GRP, 128)
        mask, tag, end = group_mask(s)
        keep = jnp.where(dstart(jnp.zeros((1, 1), F32) + (end + GRP - 1.0)) == tag, 1.0, 0.0)
        rr_ = run[...] * keep + dss[s]
        run[...] = rr_
        d = mm(rr_.astype(BF), with_ones(va[pl.ds(o, GRP), :]), 1, 1)
        dpT[:, pl.ds(o, GRP)] += jnp.where(mask, d, 0.0)
        return 0
    lax.fori_loop(0, NZ, back, 0)

    def fin(s, acc):
        o = pl.multiple_of(FRONT + GRP * s, 128)
        out = []
        for f in (0, HALF):
            pp, dd = pkT[f:f + HALF, pl.ds(o, GRP)], dpT[f:f + HALF, pl.ds(o, GRP)]
            out.append(pp * (dd - jnp.sum(pp * dd, axis=0, keepdims=True)))
        dh, dlo = hilo(jnp.concatenate(out, axis=0))
        kk = ka[pl.ds(o, GRP), :]
        return acc + mm(dh, kk) + mm(dlo, kk)
    dk = lax.fori_loop(0, NZ, fin, jnp.zeros((128, 128), F32)).T
    dq = dwq[:, :128] + dwq[:, 128:]
    dw = jnp.concatenate([dq[:, :HALF] - dq[:, HALF:], dk[:, :HALF] - dk[:, HALF:]], axis=1)
    dwb[...] = dw.reshape(NX, 32, 128)
    lx[x] = pls[...] * norm

    def scatter(i, t):
        if i:
            return rcopy(lx.at[x], lx.at[x], xs.at[1, t], xr.at[1, x], seq_1=t)
        return rcopy(dwb.at[t], wx.at[x], xs.at[0, t], xr.at[0, x], seq_1=t)
    for d in range(1, NX):
        for i in range(2):
            scatter(i, lax.rem(x + d, NX)).start()
    wx[x] = dwb[x]
    for d in range(1, NX):
        s = lax.rem(x + d, NX)
        rcopy(wx.at[s], wx.at[s], xs.at[0, s], xr.at[0, s], seq_1=s).wait_recv()
        rcopy(lx.at[s], lx.at[s], xs.at[1, s], xr.at[1, s], seq_1=s).wait_recv()
    wg[x, z] = ((wx[0] + wx[1]) + (wx[2] + wx[3])).astype(BF)
    lz[z] = (lx[0] + lx[1]) + (lx[2] + lx[3])

    def zspread(i, s, t):
        ref = (wg.at[x, s], lz.at[s])[i]
        return rcopy(ref, ref, zs.at[4 + i, t], zr.at[4 + i, s], seq_0=t)
    for j in range(1, NZ):
        for i in range(2):
            zspread(i, z, lax.rem(z + nth(j), NZ)).start()
    for j in range(1, NZ):
        s = lax.rem(z + j, NZ)
        zspread(1, s, s).wait_recv()
    part = lz[0]
    for i in range(1, NZ):
        part = part + lz[i]
    mine = NX * g + h
    lc[mine] = part
    for peer in cols:
        there = NX * peer["grp"] + peer["head"]
        rcopy(lc.at[mine], lc.at[mine], gs.at[there], gr.at[mine], **peer).start()
    for j in range(1, NZ):
        s = lax.rem(z + j, NZ)
        zspread(0, s, s).wait_recv()
    for d in range(1, NX):
        t = lax.rem(x + d, NX)
        rcopy(wg.at[x], wg.at[x], xs.at[2, t], xr.at[2, x], seq_1=t).start()
    for peer in cols:
        there = NX * peer["grp"] + peer["head"]
        rcopy(lc.at[there], lc.at[there], gs.at[there], gr.at[there], **peer).wait_recv()
    part = lc[0]
    for i in range(1, 8):
        part = part + lc[i]
    total = jnp.sum(jnp.sum(part, axis=0, keepdims=True), axis=1, keepdims=True)
    lout[...] = jnp.broadcast_to(total, (8, 128))
    keep = [pltpu.make_async_copy(tb.at[z], ta.at[z], own.at[0]),
            pltpu.make_async_copy(yb.at[z], ya.at[z], own.at[1])]
    for c in keep:
        c.start()
    for d in range(1, NX):
        s = lax.rem(x + d, NX)
        rcopy(wg.at[s], wg.at[s], xs.at[2, s], xr.at[2, s], seq_1=s).wait_recv()
    for i in range(NX):
        wout[:, i] = wg[i].astype(F32)

    def drain(j, _):
        s = lax.rem(z + j, NZ)
        for i, dst in enumerate((ta, ya)):
            rcopy(dst.at[s], dst.at[s], os.at[i, s], orr.at[i, s], seq_0=s).wait_recv()
            send_out(i, s).wait_send()
        for i in range(3):
            zcopy(i, s).wait_send()
        count_copy(s).wait_send()
        for i in range(2):
            zspread(i, z, s).wait_send()
        return 0
    lax.fori_loop(1, NZ, drain, 0)

    def drain_x(s, _):
        for i in range(2):
            xcopy(i, s, x, right, rs, rr).wait_send()
            xcopy(i, s, x, left, ls_, lr).wait_send()
        xcopy(0, s, left, right, ys, yr).wait_send()
        xcopy(1, s, right, left, ys, yr).wait_send()
        return 0
    lax.fori_loop(0, NZ, drain_x, 0)
    for d in range(1, NX):
        t = lax.rem(x + d, NX)
        scatter(0, t).wait_send()
        scatter(1, t).wait_send()
        rcopy(wg.at[x], wg.at[x], xs.at[2, t], xr.at[2, x], seq_1=t).wait_send()
    for peer in cols:
        there = NX * peer["grp"] + peer["head"]
        rcopy(lc.at[mine], lc.at[mine], gs.at[there], gr.at[mine], **peer).wait_send()
    for c in keep:
        c.wait()


def whole(norm, q, k, v, docs, fm):
    A = pl.BlockSpec(memory_space=pl.ANY)
    M = pl.BlockSpec(memory_space=pltpu.VMEM)
    D, V = pltpu.SemaphoreType.DMA, pltpu.VMEM
    return pl.pallas_call(
        functools.partial(kernel, norm),
        out_shape=(jax.ShapeDtypeStruct((NZ, BLK, 128), BF),
                   jax.ShapeDtypeStruct((NZ, BLK, 128), BF),
                   jax.ShapeDtypeStruct((NZ, NX, 32, 128), F32),
                   jax.ShapeDtypeStruct((8, 128), F32)),
        in_specs=[A, A, A, M, M], out_specs=(A, A, M, M),
        scratch_shapes=[
            V((NZ, BLK, 128), BF), V((ROWS, 128), BF), V((ROWS, 128), BF), V((NX, NZ, 8, 128), F32),
            V((NZ, BLK, 128), BF), V((ROWS, 128), BF), V((128, 256), BF), V((2, 128, 128), BF),
            V((128, ROWS), F32), V((128, ROWS), F32),
            V((NZ, BLK, 1), F32), V((NZ, BLK, 256), F32), V((NZ, BLK, 128), BF), V((NZ, BLK, 128), BF),
            V((NZ, 2, 128, 256), BF), V((NZ, 128, 256), F32), V((128, 256), F32), V((128, 256), F32),
            V((8, 128), F32),
            V((NX, 32, 128), F32), V((NX, 32, 128), F32), V((NX, NZ, 32, 128), BF),
            V((NX, 8, 128), F32), V((NZ, 8, 128), F32), V((8, 8, 128), F32),
            D((3,)), D((6, NZ)), D((6, NZ)), D((2, NZ)), D((2, NZ)), D((2, NZ)), D((2, NZ)),
            D((2, NZ)), D((2, NZ)), D((NX,)), D((NX,)), D((3, NX)), D((3, NX)), D((8,)), D((8,)),
            D((2, NZ)), D((2, NZ))],
        compiler_params=pltpu.CompilerParams(
            collective_id=0, has_side_effects=True, vmem_limit_bytes=60 << 20),
    )(q, k, v, docs, fm)


def body(queries, keys, values, documents, feature_map):
    norm = 1.0 / (TOKENS * 64)
    turned = [jnp.swapaxes(a, 0, 1) for a in (queries, keys, values)]
    ta, ya, wa, la = whole(norm, *turned, documents.reshape(1, BLK), feature_map)
    return (jnp.swapaxes(ta, 0, 1), jnp.swapaxes(ya, 0, 1), la[0, 0], wa.reshape(NZ, 128, 128))


def solution(mesh):
    split = Mesh(
        mesh.devices.reshape(mesh.shape["grp"], 8, 4, mesh.shape["head"]),
        ("grp", "seq_0", "seq_1", "head"),
    )
    return jax.shard_map(
        body,
        mesh=split,
        in_specs=(
            P(SEQ, ("grp", "head"), None),
            P(SEQ, ("grp", "head"), None),
            P(SEQ, ("grp", "head"), None),
            P(SEQ),
            P(("grp", "head"), None, None),
        ),
        out_specs=(
            P(SEQ, ("grp", "head"), None),
            P(SEQ, ("grp", "head"), None),
            P(),
            P(("grp", "head"), None, None),
        ),
        check_vma=False,
    )
```

time: 648 us -> 128 us (0.20)
  blocking collectives: 293 us -> 0 us
  waiting for transfers between devices: 161 us -> 0 us
  Pallas kernels: 0 us -> 117 us
  matrix products: 69.6 us -> 0 us
  between operations: 47.3 us -> 0.66 us
  other arithmetic: 41.7 us -> 0 us
  local copies, waits for them, and re-layouts: 18.9 us -> 7.97 us
  starting transfers between devices: 10.2 us -> 0 us
    unnamed x4 -> x0, blocking collectives: 173 us -> none
    pallas_call x0 -> x1, Pallas kernels: none -> 117 us  [whole(): pl.pallas_call(functools.partial(kernel, norm), out_shape=(jax.ShapeDtype...]
    psum x2 -> x0, waiting for transfers between devices: 97.6 us -> none  [over_axes(): return functools.reduce(lax.psum, axes, array)]
    all_gather x4 -> x0, blocking collectives: 76.9 us -> none  [carried_in(): pieces = jax.tree.map(lambda part: lax.all_gather(part, axis), subtotal)]
    dot_general x21 -> x0, matrix products: 69.6 us -> none  [the longest x1 21.6 us: body(): jnp.einsum('ihj,jhd->ihd', probabilities.astype(jnp.bfloat16), value_piec...]
    all_gather x6 -> x0, waiting for transfers between devices: 61.6 us -> none  [the longest x4 35.9 us: carried_in(): pieces = jax.tree.map(lambda part: lax.all_gather(part, axis), subtotal)]
    psum x4 -> x0, blocking collectives: 42.6 us -> none  [over_axes(): return functools.reduce(lax.psum, axes, array)]
    reduce_sum x5 -> x0, other arithmetic: 20.1 us -> none  [the longest x1 19.2 us: body(): totals = jnp.sum(probabilities, axis=-1)]
  transfers between devices with their start and end apart: 11 -> 0, of which waited for: 6 -> 0; matrix products, arithmetic and copies ran while one was open for 13% -> 0% of each run, Pallas kernels for 0% -> 0%
where the time goes in v2:
time: 128 us; the launch traced here: 126 us
  Pallas kernels  117 us (91%)
  local copies, waits for them, and re-layouts  7.97 us (6%)
    pallas_call x1, Pallas kernels, whole(): pl.pallas_call(functools.partial(kernel, norm), out_shape=(jax.ShapeDtype...  117 us
    unnamed x12, local copies, waits for them, and re-layouts  5.76 us

profile of v2, /device:TPU:32, one launch (start us, length us, event | category | flops | bytes accessed | tf_op | source)
XLA Modules:
  0.0 125.7 jit_solution(11808637303241144700)
XLA Ops:
  0.6 0.0 copy-start.2
  0.6 0.0 copy-start.3
  0.7 1.9 %copy.17 = bf16[192,8,128]{2,0,1:T(8,128)(2,1)} copy(bf16[192,8,128]{2,1,0:T(8,128)(2,1)} %param.5) | data formatting | bytes 786432 | tf_op args[0]
  2.5 0.0 copy-done.2
  2.5 0.0 copy-done.3
  2.5 1.0 copy_bitcast_fusion
  3.5 117.1 %shard_map.84 = (bf16[8,192,128]{2,1,0:T(8,128)(2,1)}, bf16[8,192,128]{2,1,0:T(8,128)(2,1)}, f32[8,4,32,128]{3,2,1,0:T(8,128)}, f32[8,128]{1,0:T(8,128)}) custom-call(bf16[8,192,128]{2,1,0:T(8,128)(2,1)} %bitcast.12, bf16[8,192,128]{2,1,0:T(8,128)(2,1)} %get-tuple-element.17.k_ref, bf16[8,192,128]{2,1,0:T(8,128)(2,1)} %get-tuple-element.16.v_ref, ...), custom_call_target="tpu_custom_call" | custom-call | tf_op jit(solution)/shard_map/pallas_call | solution.py:448
  120.7 1.2 slice.3
  121.9 0.0 copy-start.1
  121.9 2.0 %copy.12 = bf16[192,8,128]{2,1,0:T(8,128)(2,1)} copy(bf16[192,8,128]{2,0,1:T(8,128)(2,1)} %bitcast.15) | data formatting | bytes 786432
  123.9 0.0 copy-start
  123.9 0.0 copy-done.1
  123.9 1.0 copy.13
  124.9 0.0 copy-done
  124.9 0.8 copy.19
Async XLA Ops:
  0.6 1.9 %copy-start.2 = (bf16[192,8,128]{2,1,0:T(8,128)(2,1)S(1)}, bf16[192,8,128]{2,1,0:T(8,128)(2,1)}, u32[]{:S(2)}) copy-start(bf16[192,8,128]{2,1,0:T(8,128)(2,1)} %param.7) | copy-start | bytes 1179652
  0.6 1.9 %copy-start.3 = (bf16[192,8,128]{2,1,0:T(8,128)(2,1)S(1)}, bf16[192,8,128]{2,1,0:T(8,128)(2,1)}, u32[]{:S(2)}) copy-start(bf16[192,8,128]{2,1,0:T(8,128)(2,1)} %param.6) | copy-start | bytes 1179652
  121.9 2.1 %copy-start.1 = (bf16[8,192,128]{2,1,0:T(8,128)(2,1)S(1)}, bf16[8,192,128]{2,1,0:T(8,128)(2,1)}, u32[]{:S(2)}) copy-start(bf16[8,192,128]{2,1,0:T(8,128)(2,1)} %get-tuple-element.9) | copy-start | bytes 1179652
  123.9 1.0 copy-start

commit v3 on v2

--- a/solution.py
+++ b/solution.py
@@ -37,13 +37,6 @@
         device_id=where, device_id_type=MESH)
 
 
-def greet(peers):
-    barrier = pltpu.get_barrier_semaphore()
-    for peer in peers:
-        pl.semaphore_signal(barrier, inc=1, device_id=peer, device_id_type=MESH)
-    pl.semaphore_wait(barrier, len(peers))
-
-
 def nth(j):
     odd = lax.rem(j, 2)
     return lax.rem(odd * ((j + 1) // 2) + (1 - odd) * (NZ - j // 2), NZ)
@@ -58,13 +51,24 @@
 
 
 def kernel(norm, q_ref, k_ref, v_ref, doc_ref, fm_ref, ta, ya, wout, lout,
-           qa, ka, va, ca, qe, ke, wq2, wk2, pkT, dpT, ms, accs, tb, yb, sts, dss, run, dwq, pls,
+           flat, out3, tr, qa, ka, va, ca, qe, ke, wq2, wk2, pkT, dpT, ms, accs, tb, yb, sts, dss, run, dwq, pls,
            dwb, wx, wg, lx, lz, lc,
            own, zs, zr, rs, rr, ls_, lr, ys, yr, cs, cr, xs, xr, gs, gr, os, orr):
     z, x = lax.axis_index("seq_0"), lax.axis_index("seq_1")
     h, g = lax.axis_index("head"), lax.axis_index("grp")
     right, left, far = lax.rem(x + 1, NX), lax.rem(x + 3, NX), lax.rem(x + 2, NX)
     cols = [{"grp": lax.rem(g + (d // NX), 2), "head": lax.rem(h + d % NX, NX)} for d in range(1, 8)]
+
+    everyone = ([{"seq_0": lax.rem(z + d, NZ)} for d in range(1, NZ)]
+                + [{"seq_1": lax.rem(x + d, NX)} for d in range(1, NX)] + cols)
+    barrier = pltpu.get_barrier_semaphore()
+    for peer in everyone:
+        pl.semaphore_signal(barrier, inc=1, device_id=peer, device_id_type=MESH)
+
+    for i, ref in enumerate((k_ref, v_ref, q_ref)):
+        flat[...] = ref[...].astype(F32).reshape(BLK * NZ, 128)
+        for d in range(NZ):
+            out3[i, d] = flat[pl.ds(d, BLK, stride=NZ), :].astype(BF)
 
     docs = doc_ref[...]
     row = lax.broadcasted_iota(jnp.int32, (8, 128), 0)
@@ -87,14 +91,13 @@
     wk2[0] = wkh
     wk2[1] = wkl
 
-    greet([{"seq_0": lax.rem(z + d, NZ)} for d in range(1, NZ)]
-          + [{"seq_1": lax.rem(x + d, NX)} for d in range(1, NX)] + cols)
+    pl.semaphore_wait(barrier, len(everyone))
 
     def krows(arr, s, col):
         return arr.at[pl.ds(pl.multiple_of(FRONT + GRP * s + BLK * col, 64), BLK)]
 
     def zcopy(i, t):
-        src = (k_ref, v_ref, q_ref)[i].at[t]
+        src = out3.at[i, t]
         dst = qa.at[z] if i == 2 else krows((ka, va)[i], z, x)
         return rcopy(src, dst, zs.at[i, t], zr.at[i, z], seq_0=t)
 
@@ -109,9 +112,9 @@
         ref = krows((ka, va)[i], s, col)
         return rcopy(ref, ref, sems.at[i, s], semr.at[i, s], seq_1=to)
 
-    local = [pltpu.make_async_copy(k_ref.at[z], krows(ka, z, x), own.at[0]),
-             pltpu.make_async_copy(v_ref.at[z], krows(va, z, x), own.at[1]),
-             pltpu.make_async_copy(q_ref.at[z], qa.at[z], own.at[2])]
+    local = [pltpu.make_async_copy(out3.at[0, z], krows(ka, z, x), own.at[0]),
+             pltpu.make_async_copy(out3.at[1, z], krows(va, z, x), own.at[1]),
+             pltpu.make_async_copy(out3.at[2, z], qa.at[z], own.at[2])]
     for c in local:
         c.start()
     for j in range(1, NZ):
@@ -143,6 +146,9 @@
         xcopy(0, s, far, right, ys, yr).wait_recv()
         xcopy(1, s, far, left, ys, yr).wait_recv()
 
+    def nearby(n):
+        return lax.rem(z + nth(n), NZ)
+
     forward(z)
     for j in range(1, NZ):
         s = lax.rem(z + j, NZ)
@@ -151,6 +157,10 @@
         t = lax.rem(x + d, NX)
         rcopy(ca.at[x], ca.at[x], cs.at[t], cr.at[x], seq_1=t).start()
     relay(z)
+    first = nearby(1)
+    zarrive(0, first)
+    zarrive(1, first)
+    forward(first)
     for d in range(1, NX):
         s = lax.rem(x + d, NX)
         rcopy(ca.at[s], ca.at[s], cs.at[s], cr.at[s], seq_1=s).wait_recv()
@@ -176,7 +186,7 @@
         return (GRP * s + BLK * x).astype(F32) + iota((BLK, 1), 0)
 
     def absorb(n):
-        a = lax.rem(z + nth(n), NZ)
+        a = nearby(n)
         o = pl.multiple_of(FRONT + GRP * a, 128)
         kk = ka[pl.ds(o, GRP), :]
         l = mm(wk2[0], kk, 1, 1) + mm(wk2[1], kk, 1, 1)
@@ -197,36 +207,54 @@
         ms[a] = m
         accs[a] = mm(p.astype(BF), with_ones(va[pl.ds(o, GRP), :]))
 
-        def pair(j, _):
-            b = lax.rem(z + nth(j), NZ)
+        def place(j):
+            b = nearby(j)
             ge = (a - b + NZ) // NZ
             zq, zk = ge * a + (1 - ge) * b, ge * b + (1 - ge) * a
-            r = pl.multiple_of(FRONT + GRP * zk, 128)
-            sc = mm(jnp.concatenate([qa[zq], qe[zq]], axis=1),
-                    jnp.concatenate([ka[pl.ds(r, GRP), :], ke[pl.ds(r, GRP), :]], axis=1), 1, 1)
-            mo = ms[zq]
-            mn = jnp.maximum(mo, jnp.max(sc, axis=1, keepdims=True))
-            pp = jnp.exp2((sc - mn) * C2)
-            ms[zq] = mn
-            accs[zq] = accs[zq] * jnp.exp2((mo - mn) * C2) + mm(
-                pp.astype(BF), with_ones(va[pl.ds(r, GRP), :]))
+            return zq, pl.ds(pl.multiple_of(FRONT + GRP * zk, 128), GRP)
+
+        def pairs(spots):
+            scs = [mm(jnp.concatenate([qa[zq], qe[zq]], axis=1),
+                      jnp.concatenate([ka[r, :], ke[r, :]], axis=1), 1, 1) for zq, r in spots]
+            tops = [jnp.max(sc, axis=1, keepdims=True) for sc in scs]
+            olds, news = [], []
+            for (zq, _), top in zip(spots, tops):
+                olds.append(ms[zq])
+                news.append(jnp.maximum(olds[-1], top))
+                ms[zq] = news[-1]
+            sums = [mm(jnp.exp2((sc - mn) * C2).astype(BF), with_ones(va[r, :]))
+                    for sc, mn, (_, r) in zip(scs, news, spots)]
+            for (zq, _), mo, mn, add in zip(spots, olds, news, sums):
+                accs[zq] = accs[zq] * jnp.exp2((mo - mn) * C2) + add
+
+        @pl.when(lax.rem(n, 2) == 1)
+        def _():
+            pairs([place(n - 1)])
+
+        def two(j, _):
+            pairs([place(2 * j), place(2 * j + 1)])
             return 0
-        lax.fori_loop(0, n, pair, 0)
+        lax.fori_loop(0, n // 2, two, 0)
 
     def step(n, _):
-        s = lax.rem(z + nth(n), NZ)
+        s = nearby(n)
         zarrive(0, s)
         zarrive(1, s)
         forward(s)
-        prior = lax.rem(z + nth(n - 1), NZ)
-        complete(prior)
-        absorb(n - 1)
-        relay(s)
-        zarrive(2, s)
-        return 0
-    lax.fori_loop(1, NZ, step, 0)
-    complete(lax.rem(z + nth(NZ - 1), NZ))
-    absorb(jnp.int32(NZ - 1))
+        relay(nearby(n - 1))
+        complete(nearby(n - 2))
+        absorb(n - 2)
+        zarrive(2, nearby(n - 1))
+        return 0
+    lax.fori_loop(2, NZ, step, 0)
+    relay(nearby(NZ - 1))
+    zarrive(2, nearby(NZ - 1))
+
+    def late(n, _):
+        complete(nearby(n))
+        absorb(n)
+        return 0
+    lax.fori_loop(NZ - 2, NZ, late, 0)
 
     off = BLK * x + 64 * lax.rem(x, 2)
     run[...] = jnp.zeros_like(run)
@@ -260,8 +288,7 @@
     dpT[...] = jnp.zeros_like(dpT)
 
     def send_out(i, t):
-        src, dst = ((tb, ta), (yb, ya))[i]
-        return rcopy(src.at[t], dst.at[z], os.at[i, t], orr.at[i, z], seq_0=t)
+        return rcopy((tb, yb)[i].at[t], tr.at[i, z], os.at[i, t], orr.at[i, z], seq_0=t)
 
     def block(n, _):
         s = lax.rem(z + nth(NZ - 1 - n), NZ)
@@ -323,6 +350,15 @@
         return 0
     lax.fori_loop(0, NZ, block, 0)
 
+    def lscatter(t):
+        return rcopy(lx.at[x], lx.at[x], xs.at[1, t], xr.at[1, x], seq_1=t)
+
+    def lspread(s, t):
+        return rcopy(lz.at[s], lz.at[s], zs.at[5, t], zr.at[5, s], seq_0=t)
+    lx[x] = pls[...] * norm
+    for d in range(1, NX):
+        lscatter(lax.rem(x + d, NX)).start()
+
     run[...] = jnp.zeros_like(run)
 
     def back(n, _):
@@ -336,6 +372,12 @@
         dpT[:, pl.ds(o, GRP)] += jnp.where(mask, d, 0.0)
         return 0
     lax.fori_loop(0, NZ, back, 0)
+    for d in range(1, NX):
+        s = lax.rem(x + d, NX)
+        rcopy(lx.at[s], lx.at[s], xs.at[1, s], xr.at[1, s], seq_1=s).wait_recv()
+    lz[z] = (lx[0] + lx[1]) + (lx[2] + lx[3])
+    for j in range(1, NZ):
+        lspread(z, lax.rem(z + nth(j), NZ)).start()
 
     def fin(s, acc):
         o = pl.multiple_of(FRONT + GRP * s, 128)
@@ -350,32 +392,18 @@
     dq = dwq[:, :128] + dwq[:, 128:]
     dw = jnp.concatenate([dq[:, :HALF] - dq[:, HALF:], dk[:, :HALF] - dk[:, HALF:]], axis=1)
     dwb[...] = dw.reshape(NX, 32, 128)
-    lx[x] = pls[...] * norm
-
-    def scatter(i, t):
-        if i:
-            return rcopy(lx.at[x], lx.at[x], xs.at[1, t], xr.at[1, x], seq_1=t)
+
+    def scatter(t):
         return rcopy(dwb.at[t], wx.at[x], xs.at[0, t], xr.at[0, x], seq_1=t)
-    for d in range(1, NX):
-        for i in range(2):
-            scatter(i, lax.rem(x + d, NX)).start()
+
+    def zspread(s, t):
+        return rcopy(wg.at[x, s], wg.at[x, s], zs.at[4, t], zr.at[4, s], seq_0=t)
+    for d in range(1, NX):
+        scatter(lax.rem(x + d, NX)).start()
     wx[x] = dwb[x]
-    for d in range(1, NX):
-        s = lax.rem(x + d, NX)
-        rcopy(wx.at[s], wx.at[s], xs.at[0, s], xr.at[0, s], seq_1=s).wait_recv()
-        rcopy(lx.at[s], lx.at[s], xs.at[1, s], xr.at[1, s], seq_1=s).wait_recv()
-    wg[x, z] = ((wx[0] + wx[1]) + (wx[2] + wx[3])).astype(BF)
-    lz[z] = (lx[0] + lx[1]) + (lx[2] + lx[3])
-
-    def zspread(i, s, t):
-        ref = (wg.at[x, s], lz.at[s])[i]
-        return rcopy(ref, ref, zs.at[4 + i, t], zr.at[4 + i, s], seq_0=t)
-    for j in range(1, NZ):
-        for i in range(2):
-            zspread(i, z, lax.rem(z + nth(j), NZ)).start()
     for j in range(1, NZ):
         s = lax.rem(z + j, NZ)
-        zspread(1, s, s).wait_recv()
+        lspread(s, s).wait_recv()
     part = lz[0]
     for i in range(1, NZ):
         part = part + lz[i]
@@ -384,24 +412,36 @@
     for peer in cols:
         there = NX * peer["grp"] + peer["head"]
         rcopy(lc.at[mine], lc.at[mine], gs.at[there], gr.at[mine], **peer).start()
+    for d in range(1, NX):
+        s = lax.rem(x + d, NX)
+        rcopy(wx.at[s], wx.at[s], xs.at[0, s], xr.at[0, s], seq_1=s).wait_recv()
+    wg[x, z] = ((wx[0] + wx[1]) + (wx[2] + wx[3])).astype(BF)
+    for j in range(1, NZ):
+        zspread(z, lax.rem(z + nth(j), NZ)).start()
+
+    def land(i, src, dst):
+        for j in range(1, NZ):
+            s = lax.rem(z + j, NZ)
+            rcopy(tr.at[i, s], tr.at[i, s], os.at[i, s], orr.at[i, s], seq_0=s).wait_recv()
+        tr[i, z] = src[z]
+        for d in range(NZ):
+            flat[pl.ds(d, BLK, stride=NZ), :] = tr[i, d].astype(F32)
+        dst[...] = flat[...].reshape(BLK, NZ, 128).astype(BF)
+    land(0, tb, ta)
     for j in range(1, NZ):
         s = lax.rem(z + j, NZ)
-        zspread(0, s, s).wait_recv()
+        zspread(s, s).wait_recv()
     for d in range(1, NX):
         t = lax.rem(x + d, NX)
         rcopy(wg.at[x], wg.at[x], xs.at[2, t], xr.at[2, x], seq_1=t).start()
+    land(1, yb, ya)
     for peer in cols:
         there = NX * peer["grp"] + peer["head"]
         rcopy(lc.at[there], lc.at[there], gs.at[there], gr.at[there], **peer).wait_recv()
     part = lc[0]
     for i in range(1, 8):
         part = part + lc[i]
-    total = jnp.sum(jnp.sum(part, axis=0, keepdims=True), axis=1, keepdims=True)
-    lout[...] = jnp.broadcast_to(total, (8, 128))
-    keep = [pltpu.make_async_copy(tb.at[z], ta.at[z], own.at[0]),
-            pltpu.make_async_copy(yb.at[z], ya.at[z], own.at[1])]
-    for c in keep:
-        c.start()
+    lout[...] = jnp.sum(jnp.sum(part, axis=0, keepdims=True), axis=1, keepdims=True)
     for d in range(1, NX):
         s = lax.rem(x + d, NX)
         rcopy(wg.at[s], wg.at[s], xs.at[2, s], xr.at[2, s], seq_1=s).wait_recv()
@@ -410,14 +450,13 @@
 
     def drain(j, _):
         s = lax.rem(z + j, NZ)
-        for i, dst in enumerate((ta, ya)):
-            rcopy(dst.at[s], dst.at[s], os.at[i, s], orr.at[i, s], seq_0=s).wait_recv()
+        for i in range(2):
             send_out(i, s).wait_send()
         for i in range(3):
             zcopy(i, s).wait_send()
         count_copy(s).wait_send()
-        for i in range(2):
-            zspread(i, z, s).wait_send()
+        zspread(z, s).wait_send()
+        lspread(z, s).wait_send()
         return 0
     lax.fori_loop(1, NZ, drain, 0)
 
@@ -431,28 +470,26 @@
     lax.fori_loop(0, NZ, drain_x, 0)
     for d in range(1, NX):
         t = lax.rem(x + d, NX)
-        scatter(0, t).wait_send()
-        scatter(1, t).wait_send()
+        scatter(t).wait_send()
+        lscatter(t).wait_send()
         rcopy(wg.at[x], wg.at[x], xs.at[2, t], xr.at[2, x], seq_1=t).wait_send()
     for peer in cols:
         there = NX * peer["grp"] + peer["head"]
         rcopy(lc.at[mine], lc.at[mine], gs.at[there], gr.at[mine], **peer).wait_send()
-    for c in keep:
-        c.wait()
 
 
 def whole(norm, q, k, v, docs, fm):
-    A = pl.BlockSpec(memory_space=pl.ANY)
     M = pl.BlockSpec(memory_space=pltpu.VMEM)
     D, V = pltpu.SemaphoreType.DMA, pltpu.VMEM
     return pl.pallas_call(
         functools.partial(kernel, norm),
-        out_shape=(jax.ShapeDtypeStruct((NZ, BLK, 128), BF),
-                   jax.ShapeDtypeStruct((NZ, BLK, 128), BF),
+        out_shape=(jax.ShapeDtypeStruct((BLK, NZ, 128), BF),
+                   jax.ShapeDtypeStruct((BLK, NZ, 128), BF),
                    jax.ShapeDtypeStruct((NZ, NX, 32, 128), F32),
-                   jax.ShapeDtypeStruct((8, 128), F32)),
-        in_specs=[A, A, A, M, M], out_specs=(A, A, M, M),
+                   jax.ShapeDtypeStruct((1, 1), F32)),
+        in_specs=[M] * 5, out_specs=(M,) * 4,
         scratch_shapes=[
+            V((BLK * NZ, 128), F32), V((3, NZ, BLK, 128), BF), V((2, NZ, BLK, 128), BF),
             V((NZ, BLK, 128), BF), V((ROWS, 128), BF), V((ROWS, 128), BF), V((NX, NZ, 8, 128), F32),
             V((NZ, BLK, 128), BF), V((ROWS, 128), BF), V((128, 256), BF), V((2, 128, 128), BF),
             V((128, ROWS), F32), V((128, ROWS), F32),
@@ -471,9 +508,8 @@
 
 def body(queries, keys, values, documents, feature_map):
     norm = 1.0 / (TOKENS * 64)
-    turned = [jnp.swapaxes(a, 0, 1) for a in (queries, keys, values)]
-    ta, ya, wa, la = whole(norm, *turned, documents.reshape(1, BLK), feature_map)
-    return (jnp.swapaxes(ta, 0, 1), jnp.swapaxes(ya, 0, 1), la[0, 0], wa.reshape(NZ, 128, 128))
+    ta, ya, wa, la = whole(norm, queries, keys, values, documents.reshape(1, BLK), feature_map)
+    return (ta, ya, la.reshape(()), wa.reshape(NZ, 128, 128))
 
 
 def solution(mesh):

time: 128 us -> 99.9 us (0.78); the launches traced: 126 us -> 99.3 us
  Pallas kernels: 117 us -> 93.6 us
  local copies, waits for them, and re-layouts: 7.97 us -> 3.37 us
  between operations: 0.66 us -> 2.37 us
    pallas_call x1, Pallas kernels: 117 us -> 93.6 us  [whole(): pl.pallas_call(functools.partial(kernel, norm), out_shape=(jax.ShapeDtype...]
    unnamed x12 -> x7, local copies, waits for them, and re-layouts: 5.76 us -> 3.37 us
where the time goes in v3:
time: 99.9 us; the launch traced here: 99.3 us
  Pallas kernels  93.6 us (94%)
  local copies, waits for them, and re-layouts  3.37 us (3%)
  between operations  2.37 us (2%)
    pallas_call x1, Pallas kernels, whole(): pl.pallas_call(functools.partial(kernel, norm), out_shape=(jax.ShapeDtype...  93.6 us
    unnamed x7, local copies, waits for them, and re-layouts  3.37 us

profile of v3, /device:TPU:32, one launch (start us, length us, event | category | flops | bytes accessed | tf_op | source)
XLA Modules:
  0.0 99.3 jit_solution(18428403934568999782)
XLA Ops:
  0.6 93.6 %shard_map.84 = (bf16[192,8,128]{2,1,0:T(8,128)(2,1)}, bf16[192,8,128]{2,1,0:T(8,128)(2,1)}, f32[8,4,32,128]{3,2,1,0:T(8,128)}, f32[1,1]{1,0:T(1,128)}) custom-call(bf16[192,8,128]{2,1,0:T(8,128)(2,1)} %q_ref.1, bf16[192,8,128]{2,1,0:T(8,128)(2,1)} %k_ref.1, bf16[192,8,128]{2,1,0:T(8,128)(2,1)} %v_ref.1, s32[1,192]{1,0:T(1,128)} %bitcast.4, ...), custom_call_target="tpu_custom_call" | custom-call | tf_op jit(solution)/shard_map/pallas_call | solution.py:484
  94.2 0.0 copy-start.1
  94.2 1.8 %copy.13 = bf16[192,8,128]{2,1,0:T(8,128)(2,1)} copy(bf16[192,8,128]{2,1,0:T(8,128)(2,1)} %get-tuple-element.16) | data formatting | bytes 786432
  96.0 0.0 copy-done.1
  96.0 0.0 copy-start
  96.0 0.7 copy.14
  97.4 0.0 copy-done
  97.4 0.8 copy.16
Async XLA Ops:
  94.2 1.8 %copy-start.1 = (bf16[192,8,128]{2,1,0:T(8,128)(2,1)S(1)}, bf16[192,8,128]{2,1,0:T(8,128)(2,1)}, u32[]{:S(2)}) copy-start(bf16[192,8,128]{2,1,0:T(8,128)(2,1)} %get-tuple-element.17) | copy-start | bytes 1179652
  96.0 1.3 %copy-start = (f32[8,4,32,128]{3,2,1,0:T(8,128)S(1)}, f32[8,4,32,128]{3,2,1,0:T(8,128)}, u32[]{:S(2)}) copy-start(f32[8,4,32,128]{3,2,1,0:T(8,128)} %get-tuple-element.11) | copy-start | bytes 1572868

commit v4 on v3

--- a/solution.py
+++ b/solution.py
@@ -51,7 +51,7 @@
 
 
 def kernel(norm, q_ref, k_ref, v_ref, doc_ref, fm_ref, ta, ya, wout, lout,
-           flat, out3, tr, qa, ka, va, ca, qe, ke, wq2, wk2, pkT, dpT, ms, accs, tb, yb, sts, dss, run, dwq, pls,
+           flat, out3, tr, qa, ka, va, ca, qe, kT, vT, wq2, wk2, pkT, dpT, ms, accs, tb, yb, sts, dss, run, dwq, pls,
            dwb, wx, wg, lx, lz, lc,
            own, zs, zr, rs, rr, ls_, lr, ys, yr, cs, cr, xs, xr, gs, gr, os, orr):
     z, x = lax.axis_index("seq_0"), lax.axis_index("seq_1")
@@ -78,10 +78,12 @@
         tile = tile + jnp.where(row == d, jnp.broadcast_to(n, (8, 128)), 0.0)
     ca[x, z] = tile
     zero = jnp.zeros((FRONT, 128), BF)
-    ka[:FRONT] = zero
-    va[:FRONT] = zero
-    ka[FRONT + TOKENS:] = zero[:128]
-    va[FRONT + TOKENS:] = zero[:128]
+    for ref in (ka, va):
+        ref[:FRONT] = zero
+        ref[FRONT + TOKENS:] = zero[:128]
+    vT[:, :FRONT] = jnp.zeros((128, FRONT), BF)
+    vT[:, FRONT + TOKENS:] = jnp.zeros((128, 128), BF)
+    dpT[...] = jnp.zeros_like(dpT)
     pkT[:, :FRONT] = jnp.zeros((128, FRONT), F32)
     pkT[:, FRONT + TOKENS:] = jnp.zeros((128, 128), F32)
     w = fm_ref[z]
@@ -120,12 +122,19 @@
     for j in range(1, NZ):
         count_copy(lax.rem(z + nth(j), NZ)).start()
 
+    def target(j):
+        return lax.rem(z + NZ - nth(j), NZ)
+
     def send_all(j, _):
-        t = lax.rem(z + NZ - nth(j), NZ)
-        for i in range(3):
-            zcopy(i, t).start()
+        zcopy(0, target(j)).start()
+        zcopy(1, target(j)).start()
+
+        @pl.when(j > 1)
+        def _():
+            zcopy(2, target(j - 1)).start()
         return 0
     lax.fori_loop(1, NZ, send_all, 0)
+    zcopy(2, target(NZ - 1)).start()
     for c in local:
         c.wait()
 
@@ -150,17 +159,18 @@
         return lax.rem(z + nth(n), NZ)
 
     forward(z)
-    for j in range(1, NZ):
-        s = lax.rem(z + j, NZ)
-        rcopy(ca.at[x, s], ca.at[x, s], zs.at[3, s], zr.at[3, s], seq_0=s).wait_recv()
-    for d in range(1, NX):
-        t = lax.rem(x + d, NX)
-        rcopy(ca.at[x], ca.at[x], cs.at[t], cr.at[x], seq_1=t).start()
-    relay(z)
-    first = nearby(1)
-    zarrive(0, first)
-    zarrive(1, first)
-    forward(first)
+    for n in (1, 2):
+        zarrive(0, nearby(n))
+        zarrive(1, nearby(n))
+        forward(nearby(n))
+        relay(nearby(n - 1))
+        if n == 1:
+            for j in range(1, NZ):
+                s = lax.rem(z + j, NZ)
+                rcopy(ca.at[x, s], ca.at[x, s], zs.at[3, s], zr.at[3, s], seq_0=s).wait_recv()
+            for d in range(1, NX):
+                t = lax.rem(x + d, NX)
+                rcopy(ca.at[x], ca.at[x], cs.at[t], cr.at[x], seq_1=t).start()
     for d in range(1, NX):
         s = lax.rem(x + d, NX)
         rcopy(ca.at[s], ca.at[s], cs.at[s], cr.at[s], seq_1=s).wait_recv()
@@ -179,6 +189,11 @@
     high = jnp.where(lane == 0, full(1), jnp.where(lane == 1, full(2), jnp.where(
         lane == 2, full(3), 1e9)))
 
+    sub = lax.broadcasted_iota(jnp.int32, (128, 1), 0)
+    low_col = jnp.where(sub == 0, 0.0, jnp.where(sub == 1, st1, jnp.where(
+        sub == 2, st2, jnp.where(sub == 3, st3, 1e9))))
+    high_col = jnp.where(sub == 0, st1, jnp.where(sub == 1, st2, jnp.where(sub == 2, st3, 1e9)))
+
     def dstart(i):
         return jnp.where(i >= st3, st3, jnp.where(i >= st2, st2, jnp.where(i >= st1, st1, 0.0)))
 
@@ -188,19 +203,21 @@
     def absorb(n):
         a = nearby(n)
         o = pl.multiple_of(FRONT + GRP * a, 128)
-        kk = ka[pl.ds(o, GRP), :]
-        l = mm(wk2[0], kk, 1, 1) + mm(wk2[1], kk, 1, 1)
+        kk = ka[pl.ds(o, GRP), :].T
+        kT[:128, pl.ds(o, GRP)] = kk
+        vT[:, pl.ds(o, GRP)] = va[pl.ds(o, GRP), :].T
+        l = mm(wk2[0], kk) + mm(wk2[1], kk)
         for f in (0, HALF):
             lh = l[f:f + HALF]
             e = jnp.exp(lh - jnp.max(lh, axis=0, keepdims=True))
             pkT[f:f + HALF, pl.ds(o, GRP)] = e * (1.0 / jnp.sum(e, axis=0, keepdims=True))
-        kpos = (GRP * a).astype(F32) + iota((GRP, 1), 0)
-        ke[pl.ds(o, GRP), :] = jnp.where((kpos >= low) & (kpos < high), 1.0, 0.0).astype(BF)
+        kpos = (GRP * a).astype(F32) + iota((1, GRP), 1)
+        kT[128:, pl.ds(o, GRP)] = jnp.where((kpos >= low_col) & (kpos < high_col), 1.0, 0.0).astype(BF)
         icol = qpos(a)
         miss = jnp.logical_not((icol >= low) & (icol < high)) & (lane < 4)
         qe[a] = jnp.where(miss, NEG, 0.0).astype(BF)
         jrow = (GRP * a).astype(F32) + iota((1, GRP), 1)
-        s = mm(qa[a], kk, 1, 1)
+        s = mm(qa[a], kk)
         s = jnp.where((jrow <= icol) & (jrow >= dstart(icol)), s, NEG)
         m = jnp.max(s, axis=1, keepdims=True)
         p = jnp.exp2((s - m) * C2)
@@ -215,7 +232,7 @@
 
         def pairs(spots):
             scs = [mm(jnp.concatenate([qa[zq], qe[zq]], axis=1),
-                      jnp.concatenate([ka[r, :], ke[r, :]], axis=1), 1, 1) for zq, r in spots]
+                      kT[:, r]) for zq, r in spots]
             tops = [jnp.max(sc, axis=1, keepdims=True) for sc in scs]
             olds, news = [], []
             for (zq, _), top in zip(spots, tops):
@@ -237,24 +254,29 @@
         lax.fori_loop(0, n // 2, two, 0)
 
     def step(n, _):
-        s = nearby(n)
+        complete(nearby(n - 2))
+        absorb(n - 2)
+        s = nearby(n + 1)
         zarrive(0, s)
         zarrive(1, s)
         forward(s)
-        relay(nearby(n - 1))
-        complete(nearby(n - 2))
-        absorb(n - 2)
+        relay(nearby(n))
         zarrive(2, nearby(n - 1))
         return 0
-    lax.fori_loop(2, NZ, step, 0)
-    relay(nearby(NZ - 1))
-    zarrive(2, nearby(NZ - 1))
+    lax.fori_loop(2, NZ - 1, step, 0)
 
     def late(n, _):
+        @pl.when(n > NZ - 3)
+        def _():
+            zarrive(2, nearby(n))
         complete(nearby(n))
         absorb(n)
-        return 0
-    lax.fori_loop(NZ - 2, NZ, late, 0)
+
+        @pl.when(n == NZ - 3)
+        def _():
+            relay(nearby(NZ - 1))
+        return 0
+    lax.fori_loop(NZ - 3, NZ, late, 0)
 
     off = BLK * x + 64 * lax.rem(x, 2)
     run[...] = jnp.zeros_like(run)
@@ -285,7 +307,6 @@
 
     dwq[...] = jnp.zeros_like(dwq)
     pls[...] = jnp.zeros_like(pls)
-    dpT[...] = jnp.zeros_like(dpT)
 
     def send_out(i, t):
         return rcopy((tb, yb)[i].at[t], tr.at[i, z], os.at[i, t], orr.at[i, z], seq_0=t)
@@ -368,7 +389,7 @@
         keep = jnp.where(dstart(jnp.zeros((1, 1), F32) + (end + GRP - 1.0)) == tag, 1.0, 0.0)
         rr_ = run[...] * keep + dss[s]
         run[...] = rr_
-        d = mm(rr_.astype(BF), with_ones(va[pl.ds(o, GRP), :]), 1, 1)
+        d = mm(rr_.astype(BF), jnp.concatenate([vT[:, pl.ds(o, GRP)], jnp.ones((128, GRP), BF)], axis=0))
         dpT[:, pl.ds(o, GRP)] += jnp.where(mask, d, 0.0)
         return 0
     lax.fori_loop(0, NZ, back, 0)
@@ -491,7 +512,7 @@
         scratch_shapes=[
             V((BLK * NZ, 128), F32), V((3, NZ, BLK, 128), BF), V((2, NZ, BLK, 128), BF),
             V((NZ, BLK, 128), BF), V((ROWS, 128), BF), V((ROWS, 128), BF), V((NX, NZ, 8, 128), F32),
-            V((NZ, BLK, 128), BF), V((ROWS, 128), BF), V((128, 256), BF), V((2, 128, 128), BF),
+            V((NZ, BLK, 128), BF), V((256, ROWS), BF), V((128, ROWS), BF), V((128, 256), BF), V((2, 128, 128), BF),
             V((128, ROWS), F32), V((128, ROWS), F32),
             V((NZ, BLK, 1), F32), V((NZ, BLK, 256), F32), V((NZ, BLK, 128), BF), V((NZ, BLK, 128), BF),
             V((NZ, 2, 128, 256), BF), V((NZ, 128, 256), F32), V((128, 256), F32), V((128, 256), F32),

time: 99.9 us -> 98.8 us (0.989)
  no operation moved by 1% of the time
where the time goes in v4:
time: 98.8 us; the launch traced here: 98.6 us
  Pallas kernels  92.9 us (94%)
  local copies, waits for them, and re-layouts  3.37 us (3%)
  between operations  2.37 us (2%)
    pallas_call x1, Pallas kernels, whole(): pl.pallas_call(functools.partial(kernel, norm), out_shape=(jax.ShapeDtype...  92.9 us
    unnamed x7, local copies, waits for them, and re-layouts  3.37 us

profile of v4, /device:TPU:32, one launch (start us, length us, event | category | flops | bytes accessed | tf_op | source)
XLA Modules:
  0.0 98.6 jit_solution(14658447771646738023)
XLA Ops:
  0.6 92.9 %shard_map.84 = (bf16[192,8,128]{2,1,0:T(8,128)(2,1)}, bf16[192,8,128]{2,1,0:T(8,128)(2,1)}, f32[8,4,32,128]{3,2,1,0:T(8,128)}, f32[1,1]{1,0:T(1,128)}) custom-call(bf16[192,8,128]{2,1,0:T(8,128)(2,1)} %q_ref.1, bf16[192,8,128]{2,1,0:T(8,128)(2,1)} %k_ref.1, bf16[192,8,128]{2,1,0:T(8,128)(2,1)} %v_ref.1, s32[1,192]{1,0:T(1,128)} %bitcast.4, ...), custom_call_target="tpu_custom_call" | custom-call | tf_op jit(solution)/shard_map/pallas_call | solution.py:505
  93.5 0.0 copy-start.1
  93.5 1.8 %copy.13 = bf16[192,8,128]{2,1,0:T(8,128)(2,1)} copy(bf16[192,8,128]{2,1,0:T(8,128)(2,1)} %get-tuple-element.16) | data formatting | bytes 786432
  95.3 0.0 copy-done.1
  95.3 0.0 copy-start
  95.4 0.7 copy.14
  96.7 0.0 copy-done
  96.7 0.8 copy.16
Async XLA Ops:
  93.5 1.8 %copy-start.1 = (bf16[192,8,128]{2,1,0:T(8,128)(2,1)S(1)}, bf16[192,8,128]{2,1,0:T(8,128)(2,1)}, u32[]{:S(2)}) copy-start(bf16[192,8,128]{2,1,0:T(8,128)(2,1)} %get-tuple-element.17) | copy-start | bytes 1179652
  95.3 1.3 %copy-start = (f32[8,4,32,128]{3,2,1,0:T(8,128)S(1)}, f32[8,4,32,128]{3,2,1,0:T(8,128)}, u32[]{:S(2)}) copy-start(f32[8,4,32,128]{3,2,1,0:T(8,128)} %get-tuple-element.11) | copy-start | bytes 1572868

commit v5 on v4

--- a/solution.py
+++ b/solution.py
@@ -422,6 +422,12 @@
     for d in range(1, NX):
         scatter(lax.rem(x + d, NX)).start()
     wx[x] = dwb[x]
+    for d in range(1, NX):
+        s = lax.rem(x + d, NX)
+        rcopy(wx.at[s], wx.at[s], xs.at[0, s], xr.at[0, s], seq_1=s).wait_recv()
+    wg[x, z] = ((wx[0] + wx[1]) + (wx[2] + wx[3])).astype(BF)
+    for j in range(1, NZ):
+        zspread(z, lax.rem(z + nth(j), NZ)).start()
     for j in range(1, NZ):
         s = lax.rem(z + j, NZ)
         lspread(s, s).wait_recv()
@@ -433,12 +439,6 @@
     for peer in cols:
         there = NX * peer["grp"] + peer["head"]
         rcopy(lc.at[mine], lc.at[mine], gs.at[there], gr.at[mine], **peer).start()
-    for d in range(1, NX):
-        s = lax.rem(x + d, NX)
-        rcopy(wx.at[s], wx.at[s], xs.at[0, s], xr.at[0, s], seq_1=s).wait_recv()
-    wg[x, z] = ((wx[0] + wx[1]) + (wx[2] + wx[3])).astype(BF)
-    for j in range(1, NZ):
-        zspread(z, lax.rem(z + nth(j), NZ)).start()
 
     def land(i, src, dst):
         for j in range(1, NZ):
@@ -504,9 +504,7 @@
     D, V = pltpu.SemaphoreType.DMA, pltpu.VMEM
     return pl.pallas_call(
         functools.partial(kernel, norm),
-        out_shape=(jax.ShapeDtypeStruct((BLK, NZ, 128), BF),
-                   jax.ShapeDtypeStruct((BLK, NZ, 128), BF),
-                   jax.ShapeDtypeStruct((NZ, NX, 32, 128), F32),
+        out_shape=(V((BLK, NZ, 128), BF), V((BLK, NZ, 128), BF), V((NZ, NX, 32, 128), F32),
                    jax.ShapeDtypeStruct((1, 1), F32)),
         in_specs=[M] * 5, out_specs=(M,) * 4,
         scratch_shapes=[

time: 98.8 us -> 97.1 us (0.983)
  local copies, waits for them, and re-layouts: 3.37 us -> 2.29 us
    unnamed x7 -> x3, local copies, waits for them, and re-layouts: 3.37 us -> 2.29 us
where the time goes in v5:
time: 97.1 us; the launch traced here: 96.9 us
  Pallas kernels  92.3 us (95%)
  between operations  2.33 us (2%)
  local copies, waits for them, and re-layouts  2.29 us (2%)
    pallas_call x1, Pallas kernels, whole(): pl.pallas_call(functools.partial(kernel, norm), out_shape=(V((BLK, NZ, 12...  92.3 us
    unnamed x3, local copies, waits for them, and re-layouts  2.29 us

profile of v5, /device:TPU:32, one launch (start us, length us, event | category | flops | bytes accessed | tf_op | source)
XLA Modules:
  0.0 96.9 jit_solution(13162702874043728296)
XLA Ops:
  0.6 92.3 %shard_map.84 = (bf16[192,8,128]{2,1,0:T(8,128)(2,1)S(1)}, bf16[192,8,128]{2,1,0:T(8,128)(2,1)S(1)}, f32[8,4,32,128]{3,2,1,0:T(8,128)S(1)}, f32[1,1]{1,0:T(1,128)}) custom-call(bf16[192,8,128]{2,1,0:T(8,128)(2,1)} %q_ref.1, bf16[192,8,128]{2,1,0:T(8,128)(2,1)} %k_ref.1, bf16[192,8,128]{2,1,0:T(8,128)(2,1)} %v_ref.1, s32[1,192]{1,0:T(1,128)} %bitcast.4, ...), custom_call_target="tpu_custom_call" | custom-call | tf_op jit(solution)/shard_map/pallas_call | solution.py:505
  93.0 0.7 copy.13
  93.7 0.7 copy.14
  94.5 0.8 copy.15

commit v6 on v5

--- a/solution.py
+++ b/solution.py
@@ -19,7 +19,8 @@
 F32, BF = jnp.float32, jnp.bfloat16
 NEG = -1e30
 SCALE = 128**-0.5
-C2 = SCALE * math.log2(math.e)
+LOG2E = math.log2(math.e)
+C2 = SCALE * LOG2E
 
 
 def mm(a, b, ca=1, cb=0):
@@ -51,7 +52,7 @@
 
 
 def kernel(norm, q_ref, k_ref, v_ref, doc_ref, fm_ref, ta, ya, wout, lout,
-           flat, out3, tr, qa, ka, va, ca, qe, kT, vT, wq2, wk2, pkT, dpT, ms, accs, tb, yb, sts, dss, run, dwq, pls,
+           flat, out3, tr, qa, ka, va, ca, qe, pqs, kT, vT, wq2, wk2, pkT, dpT, ms, accs, tb, yb, sts, dss, run, dwq, pls,
            dwb, wx, wg, lx, lz, lc,
            own, zs, zr, rs, rr, ls_, lr, ys, yr, cs, cr, xs, xr, gs, gr, os, orr):
     z, x = lax.axis_index("seq_0"), lax.axis_index("seq_1")
@@ -84,12 +85,13 @@
     vT[:, :FRONT] = jnp.zeros((128, FRONT), BF)
     vT[:, FRONT + TOKENS:] = jnp.zeros((128, 128), BF)
     dpT[...] = jnp.zeros_like(dpT)
+    kT[144:] = jnp.zeros((112, ROWS), BF)
     pkT[:, :FRONT] = jnp.zeros((128, FRONT), F32)
     pkT[:, FRONT + TOKENS:] = jnp.zeros((128, 128), F32)
     w = fm_ref[z]
-    wqh, wql = hilo(jnp.concatenate([w[:, :HALF], -w[:, :HALF]], axis=1))
+    wqh, wql = hilo(jnp.concatenate([w[:, :HALF], -w[:, :HALF]], axis=1) * LOG2E)
     wq2[...] = jnp.concatenate([wqh, wql], axis=1)
-    wkh, wkl = hilo(jnp.concatenate([w[:, HALF:], -w[:, HALF:]], axis=1).T)
+    wkh, wkl = hilo(jnp.concatenate([w[:, HALF:], -w[:, HALF:]], axis=1).T * LOG2E)
     wk2[0] = wkh
     wk2[1] = wkl
 
@@ -189,7 +191,7 @@
     high = jnp.where(lane == 0, full(1), jnp.where(lane == 1, full(2), jnp.where(
         lane == 2, full(3), 1e9)))
 
-    sub = lax.broadcasted_iota(jnp.int32, (128, 1), 0)
+    sub = lax.broadcasted_iota(jnp.int32, (16, 1), 0)
     low_col = jnp.where(sub == 0, 0.0, jnp.where(sub == 1, st1, jnp.where(
         sub == 2, st2, jnp.where(sub == 3, st3, 1e9))))
     high_col = jnp.where(sub == 0, st1, jnp.where(sub == 1, st2, jnp.where(sub == 2, st3, 1e9)))
@@ -209,13 +211,19 @@
         l = mm(wk2[0], kk) + mm(wk2[1], kk)
         for f in (0, HALF):
             lh = l[f:f + HALF]
-            e = jnp.exp(lh - jnp.max(lh, axis=0, keepdims=True))
+            e = jnp.exp2(lh - jnp.max(lh, axis=0, keepdims=True))
             pkT[f:f + HALF, pl.ds(o, GRP)] = e * (1.0 / jnp.sum(e, axis=0, keepdims=True))
         kpos = (GRP * a).astype(F32) + iota((1, GRP), 1)
-        kT[128:, pl.ds(o, GRP)] = jnp.where((kpos >= low_col) & (kpos < high_col), 1.0, 0.0).astype(BF)
+        kT[128:144, pl.ds(o, GRP)] = jnp.where((kpos >= low_col) & (kpos < high_col), 1.0, 0.0).astype(BF)
         icol = qpos(a)
         miss = jnp.logical_not((icol >= low) & (icol < high)) & (lane < 4)
         qe[a] = jnp.where(miss, NEG, 0.0).astype(BF)
+        lq = mm(qa[a], wq2[...])
+        lq = lq[:, :128] + lq[:, 128:]
+        for f in (0, HALF):
+            lh = lq[:, f:f + HALF]
+            e = jnp.exp2(lh - jnp.max(lh, axis=1, keepdims=True))
+            pqs[a, :, f:f + HALF] = e * (1.0 / jnp.sum(e, axis=1, keepdims=True))
         jrow = (GRP * a).astype(F32) + iota((1, GRP), 1)
         s = mm(qa[a], kk)
         s = jnp.where((jrow <= icol) & (jrow >= dstart(icol)), s, NEG)
@@ -244,6 +252,10 @@
             for (zq, _), mo, mn, add in zip(spots, olds, news, sums):
                 accs[zq] = accs[zq] * jnp.exp2((mo - mn) * C2) + add
 
+        @pl.when(n == NZ - 2)
+        def _():
+            relay(nearby(NZ - 1))
+
         @pl.when(lax.rem(n, 2) == 1)
         def _():
             pairs([place(n - 1)])
@@ -254,29 +266,24 @@
         lax.fori_loop(0, n // 2, two, 0)
 
     def step(n, _):
-        complete(nearby(n - 2))
-        absorb(n - 2)
-        s = nearby(n + 1)
-        zarrive(0, s)
-        zarrive(1, s)
-        forward(s)
-        relay(nearby(n))
-        zarrive(2, nearby(n - 1))
-        return 0
-    lax.fori_loop(2, NZ - 1, step, 0)
-
-    def late(n, _):
-        @pl.when(n > NZ - 3)
+        @pl.when(n > 0)
         def _():
             zarrive(2, nearby(n))
         complete(nearby(n))
         absorb(n)
 
-        @pl.when(n == NZ - 3)
-        def _():
-            relay(nearby(NZ - 1))
-        return 0
-    lax.fori_loop(NZ - 3, NZ, late, 0)
+        @pl.when(n < NZ - 3)
+        def _():
+            relay(nearby(n + 2))
+
+        @pl.when((n < NZ - 4) | (n == NZ - 3))
+        def _():
+            s = nearby(n + 3 - n // (NZ - 3))
+            zarrive(0, s)
+            zarrive(1, s)
+            forward(s)
+        return 0
+    lax.fori_loop(0, NZ, step, 0)
 
     off = BLK * x + 64 * lax.rem(x, 2)
     run[...] = jnp.zeros_like(run)
@@ -330,14 +337,7 @@
         jrow = (GRP * s + off + GRP - FRONT).astype(F32) + iota((1, LOC), 1)
         same = jrow >= dcol
         sc = mm(q, kl, 1, 1)
-        lq = mm(q, wq2[...])
-        lq = lq[:, :128] + lq[:, 128:]
-        ph = []
-        for f in (0, HALF):
-            lh = lq[:, f:f + HALF]
-            e = jnp.exp(lh - jnp.max(lh, axis=1, keepdims=True))
-            ph.append(e * (1.0 / jnp.sum(e, axis=1, keepdims=True)))
-        pq = jnp.concatenate(ph, axis=1)
+        pq = pqs[s]
         pq_h, pq_l = hilo(pq)
         _, tag, end = group_mask(s)
         uses = jnp.where((dcol == tag) & (end > 0.0), 1.0, 0.0)
@@ -510,7 +510,7 @@
         scratch_shapes=[
             V((BLK * NZ, 128), F32), V((3, NZ, BLK, 128), BF), V((2, NZ, BLK, 128), BF),
             V((NZ, BLK, 128), BF), V((ROWS, 128), BF), V((ROWS, 128), BF), V((NX, NZ, 8, 128), F32),
-            V((NZ, BLK, 128), BF), V((256, ROWS), BF), V((128, ROWS), BF), V((128, 256), BF), V((2, 128, 128), BF),
+            V((NZ, BLK, 128), BF), V((NZ, BLK, 128), F32), V((256, ROWS), BF), V((128, ROWS), BF), V((128, 256), BF), V((2, 128, 128), BF),
             V((128, ROWS), F32), V((128, ROWS), F32),
             V((NZ, BLK, 1), F32), V((NZ, BLK, 256), F32), V((NZ, BLK, 128), BF), V((NZ, BLK, 128), BF),
             V((NZ, 2, 128, 256), BF), V((NZ, 128, 256), F32), V((128, 256), F32), V((128, 256), F32),

time: 97.1 us -> 102 us (1.050)
  Pallas kernels: 92.3 us -> 96.8 us
    pallas_call x1, Pallas kernels: 92.3 us -> 96.8 us  [whole(): pl.pallas_call(functools.partial(kernel, norm), out_shape=(V((BLK, NZ, 12...]
where the time goes in v6:
time: 102 us; the launch traced here: 101 us
  Pallas kernels  96.8 us (95%)
  between operations  2.33 us (2%)
  local copies, waits for them, and re-layouts  2.29 us (2%)
    pallas_call x1, Pallas kernels, whole(): pl.pallas_call(functools.partial(kernel, norm), out_shape=(V((BLK, NZ, 12...  96.8 us
    unnamed x3, local copies, waits for them, and re-layouts  2.29 us

profile of v6, /device:TPU:32, one launch (start us, length us, event | category | flops | bytes accessed | tf_op | source)
XLA Modules:
  0.0 101.4 jit_solution(11927526400161899588)
XLA Ops:
  0.6 96.8 %shard_map.84 = (bf16[192,8,128]{2,1,0:T(8,128)(2,1)S(1)}, bf16[192,8,128]{2,1,0:T(8,128)(2,1)S(1)}, f32[8,4,32,128]{3,2,1,0:T(8,128)S(1)}, f32[1,1]{1,0:T(1,128)}) custom-call(bf16[192,8,128]{2,1,0:T(8,128)(2,1)} %q_ref.1, bf16[192,8,128]{2,1,0:T(8,128)(2,1)} %k_ref.1, bf16[192,8,128]{2,1,0:T(8,128)(2,1)} %v_ref.1, s32[1,192]{1,0:T(1,128)} %bitcast.4, ...), custom_call_target="tpu_custom_call" | custom-call | tf_op jit(solution)/shard_map/pallas_call | solution.py:505
  97.5 0.7 copy.13
  98.2 0.7 copy.14
  99.0 0.8 copy.15

commit v7 on v5

--- a/solution.py
+++ b/solution.py
@@ -19,7 +19,8 @@
 F32, BF = jnp.float32, jnp.bfloat16
 NEG = -1e30
 SCALE = 128**-0.5
-C2 = SCALE * math.log2(math.e)
+LOG2E = math.log2(math.e)
+C2 = SCALE * LOG2E
 
 
 def mm(a, b, ca=1, cb=0):
@@ -84,12 +85,13 @@
     vT[:, :FRONT] = jnp.zeros((128, FRONT), BF)
     vT[:, FRONT + TOKENS:] = jnp.zeros((128, 128), BF)
     dpT[...] = jnp.zeros_like(dpT)
+    kT[144:] = jnp.zeros((112, ROWS), BF)
     pkT[:, :FRONT] = jnp.zeros((128, FRONT), F32)
     pkT[:, FRONT + TOKENS:] = jnp.zeros((128, 128), F32)
     w = fm_ref[z]
-    wqh, wql = hilo(jnp.concatenate([w[:, :HALF], -w[:, :HALF]], axis=1))
+    wqh, wql = hilo(jnp.concatenate([w[:, :HALF], -w[:, :HALF]], axis=1) * LOG2E)
     wq2[...] = jnp.concatenate([wqh, wql], axis=1)
-    wkh, wkl = hilo(jnp.concatenate([w[:, HALF:], -w[:, HALF:]], axis=1).T)
+    wkh, wkl = hilo(jnp.concatenate([w[:, HALF:], -w[:, HALF:]], axis=1).T * LOG2E)
     wk2[0] = wkh
     wk2[1] = wkl
 
@@ -189,7 +191,7 @@
     high = jnp.where(lane == 0, full(1), jnp.where(lane == 1, full(2), jnp.where(
         lane == 2, full(3), 1e9)))
 
-    sub = lax.broadcasted_iota(jnp.int32, (128, 1), 0)
+    sub = lax.broadcasted_iota(jnp.int32, (16, 1), 0)
     low_col = jnp.where(sub == 0, 0.0, jnp.where(sub == 1, st1, jnp.where(
         sub == 2, st2, jnp.where(sub == 3, st3, 1e9))))
     high_col = jnp.where(sub == 0, st1, jnp.where(sub == 1, st2, jnp.where(sub == 2, st3, 1e9)))
@@ -209,10 +211,10 @@
         l = mm(wk2[0], kk) + mm(wk2[1], kk)
         for f in (0, HALF):
             lh = l[f:f + HALF]
-            e = jnp.exp(lh - jnp.max(lh, axis=0, keepdims=True))
+            e = jnp.exp2(lh - jnp.max(lh, axis=0, keepdims=True))
             pkT[f:f + HALF, pl.ds(o, GRP)] = e * (1.0 / jnp.sum(e, axis=0, keepdims=True))
         kpos = (GRP * a).astype(F32) + iota((1, GRP), 1)
-        kT[128:, pl.ds(o, GRP)] = jnp.where((kpos >= low_col) & (kpos < high_col), 1.0, 0.0).astype(BF)
+        kT[128:144, pl.ds(o, GRP)] = jnp.where((kpos >= low_col) & (kpos < high_col), 1.0, 0.0).astype(BF)
         icol = qpos(a)
         miss = jnp.logical_not((icol >= low) & (icol < high)) & (lane < 4)
         qe[a] = jnp.where(miss, NEG, 0.0).astype(BF)
@@ -248,10 +250,14 @@
         def _():
             pairs([place(n - 1)])
 
-        def two(j, _):
-            pairs([place(2 * j), place(2 * j + 1)])
+        @pl.when(lax.rem(n, 4) > 1)
+        def _():
+            pairs([place(n // 4 * 4), place(n // 4 * 4 + 1)])
+
+        def four(j, _):
+            pairs([place(4 * j + i) for i in range(4)])
             return 0
-        lax.fori_loop(0, n // 2, two, 0)
+        lax.fori_loop(0, n // 4, four, 0)
 
     def step(n, _):
         complete(nearby(n - 2))
@@ -335,7 +341,7 @@
         ph = []
         for f in (0, HALF):
             lh = lq[:, f:f + HALF]
-            e = jnp.exp(lh - jnp.max(lh, axis=1, keepdims=True))
+            e = jnp.exp2(lh - jnp.max(lh, axis=1, keepdims=True))
             ph.append(e * (1.0 / jnp.sum(e, axis=1, keepdims=True)))
         pq = jnp.concatenate(ph, axis=1)
         pq_h, pq_l = hilo(pq)

time: 97.1 us -> 95.8 us (0.987)
  Pallas kernels: 92.3 us -> 90.7 us
    pallas_call x1, Pallas kernels: 92.3 us -> 90.7 us  [whole(): pl.pallas_call(functools.partial(kernel, norm), out_shape=(V((BLK, NZ, 12...]
where the time goes in v7:
time: 95.8 us; the launch traced here: 95.3 us
  Pallas kernels  90.7 us (95%)
  between operations  2.33 us (2%)
  local copies, waits for them, and re-layouts  2.29 us (2%)
    pallas_call x1, Pallas kernels, whole(): pl.pallas_call(functools.partial(kernel, norm), out_shape=(V((BLK, NZ, 12...  90.7 us
    unnamed x3, local copies, waits for them, and re-layouts  2.29 us

profile of v7, /device:TPU:32, one launch (start us, length us, event | category | flops | bytes accessed | tf_op | source)
XLA Modules:
  0.0 95.3 jit_solution(6749143112569129151)
XLA Ops:
  0.6 90.7 %shard_map.84 = (bf16[192,8,128]{2,1,0:T(8,128)(2,1)S(1)}, bf16[192,8,128]{2,1,0:T(8,128)(2,1)S(1)}, f32[8,4,32,128]{3,2,1,0:T(8,128)S(1)}, f32[1,1]{1,0:T(1,128)}) custom-call(bf16[192,8,128]{2,1,0:T(8,128)(2,1)} %q_ref.1, bf16[192,8,128]{2,1,0:T(8,128)(2,1)} %k_ref.1, bf16[192,8,128]{2,1,0:T(8,128)(2,1)} %v_ref.1, s32[1,192]{1,0:T(1,128)} %bitcast.4, ...), custom_call_target="tpu_custom_call" | custom-call | tf_op jit(solution)/shard_map/pallas_call | solution.py:511
  91.3 0.7 copy.13
  92.1 0.7 copy.14
  92.8 0.8 copy.15

commit v8 on v7

--- a/solution.py
+++ b/solution.py
@@ -54,7 +54,7 @@
 def kernel(norm, q_ref, k_ref, v_ref, doc_ref, fm_ref, ta, ya, wout, lout,
            flat, out3, tr, qa, ka, va, ca, qe, kT, vT, wq2, wk2, pkT, dpT, ms, accs, tb, yb, sts, dss, run, dwq, pls,
            dwb, wx, wg, lx, lz, lc,
-           own, zs, zr, rs, rr, ls_, lr, ys, yr, cs, cr, xs, xr, gs, gr, os, orr):
+           own, zs, zr, rs, rr, ls_, lr, ys, yr, cs, cr, xs, xr, gs, gr, os, orr, ws, wr):
     z, x = lax.axis_index("seq_0"), lax.axis_index("seq_1")
     h, g = lax.axis_index("head"), lax.axis_index("grp")
     right, left, far = lax.rem(x + 1, NX), lax.rem(x + 3, NX), lax.rem(x + 2, NX)
@@ -425,6 +425,8 @@
 
     def zspread(s, t):
         return rcopy(wg.at[x, s], wg.at[x, s], zs.at[4, t], zr.at[4, s], seq_0=t)
+    def onward(s, t):
+        return rcopy(wg.at[x, s], wg.at[x, s], ws.at[s, t], wr.at[s, x], seq_1=t)
     for d in range(1, NX):
         scatter(lax.rem(x + d, NX)).start()
     wx[x] = dwb[x]
@@ -434,6 +436,8 @@
     wg[x, z] = ((wx[0] + wx[1]) + (wx[2] + wx[3])).astype(BF)
     for j in range(1, NZ):
         zspread(z, lax.rem(z + nth(j), NZ)).start()
+    for d in range(1, NX):
+        onward(z, lax.rem(x + d, NX)).start()
     for j in range(1, NZ):
         s = lax.rem(z + j, NZ)
         lspread(s, s).wait_recv()
@@ -456,11 +460,10 @@
         dst[...] = flat[...].reshape(BLK, NZ, 128).astype(BF)
     land(0, tb, ta)
     for j in range(1, NZ):
-        s = lax.rem(z + j, NZ)
+        s = lax.rem(z + nth(j), NZ)
         zspread(s, s).wait_recv()
-    for d in range(1, NX):
-        t = lax.rem(x + d, NX)
-        rcopy(wg.at[x], wg.at[x], xs.at[2, t], xr.at[2, x], seq_1=t).start()
+        for d in range(1, NX):
+            onward(s, lax.rem(x + d, NX)).start()
     land(1, yb, ya)
     for peer in cols:
         there = NX * peer["grp"] + peer["head"]
@@ -471,7 +474,8 @@
     lout[...] = jnp.sum(jnp.sum(part, axis=0, keepdims=True), axis=1, keepdims=True)
     for d in range(1, NX):
         s = lax.rem(x + d, NX)
-        rcopy(wg.at[s], wg.at[s], xs.at[2, s], xr.at[2, s], seq_1=s).wait_recv()
+        for j in range(NZ):
+            rcopy(wg.at[s, j], wg.at[s, j], ws.at[j, s], wr.at[j, s], seq_1=s).wait_recv()
     for i in range(NX):
         wout[:, i] = wg[i].astype(F32)
 
@@ -499,7 +503,8 @@
         t = lax.rem(x + d, NX)
         scatter(t).wait_send()
         lscatter(t).wait_send()
-        rcopy(wg.at[x], wg.at[x], xs.at[2, t], xr.at[2, x], seq_1=t).wait_send()
+        for j in range(NZ):
+            onward(j, t).wait_send()
     for peer in cols:
         there = NX * peer["grp"] + peer["head"]
         rcopy(lc.at[mine], lc.at[mine], gs.at[there], gr.at[mine], **peer).wait_send()
@@ -525,7 +530,7 @@
             V((NX, 8, 128), F32), V((NZ, 8, 128), F32), V((8, 8, 128), F32),
             D((3,)), D((6, NZ)), D((6, NZ)), D((2, NZ)), D((2, NZ)), D((2, NZ)), D((2, NZ)),
             D((2, NZ)), D((2, NZ)), D((NX,)), D((NX,)), D((3, NX)), D((3, NX)), D((8,)), D((8,)),
-            D((2, NZ)), D((2, NZ))],
+            D((2, NZ)), D((2, NZ)), D((NZ, NX)), D((NZ, NX))],
         compiler_params=pltpu.CompilerParams(
             collective_id=0, has_side_effects=True, vmem_limit_bytes=60 << 20),
     )(q, k, v, docs, fm)

time: 95.8 us -> 95.6 us (level)
  no operation moved by 1% of the time
where the time goes in v8:
time: 95.6 us; the launch traced here: 95.5 us
  Pallas kernels  90.9 us (95%)
  between operations  2.33 us (2%)
  local copies, waits for them, and re-layouts  2.29 us (2%)
    pallas_call x1, Pallas kernels, whole(): pl.pallas_call(functools.partial(kernel, norm), out_shape=(V((BLK, NZ, 12...  90.9 us
    unnamed x3, local copies, waits for them, and re-layouts  2.29 us

profile of v8, /device:TPU:32, one launch (start us, length us, event | category | flops | bytes accessed | tf_op | source)
XLA Modules:
  0.0 95.5 jit_solution(14561080105943867661)
XLA Ops:
  0.6 90.9 %shard_map.84 = (bf16[192,8,128]{2,1,0:T(8,128)(2,1)S(1)}, bf16[192,8,128]{2,1,0:T(8,128)(2,1)S(1)}, f32[8,4,32,128]{3,2,1,0:T(8,128)S(1)}, f32[1,1]{1,0:T(1,128)}) custom-call(bf16[192,8,128]{2,1,0:T(8,128)(2,1)} %q_ref.1, bf16[192,8,128]{2,1,0:T(8,128)(2,1)} %k_ref.1, bf16[192,8,128]{2,1,0:T(8,128)(2,1)} %v_ref.1, s32[1,192]{1,0:T(1,128)} %bitcast.4, ...), custom_call_target="tpu_custom_call" | custom-call | tf_op jit(solution)/shard_map/pallas_call | solution.py:516
  91.5 0.7 copy.13
  92.2 0.7 copy.14
  93.0 0.8 copy.15
